TPU v7x, 32 devices: a whole 2x2x4 slice. The times are simulated.
32 devices in a mesh: depth: 8 (over y, x, core), tile: 4 (over z).
Axes of the slice: x: 2, y: 2, z: 4, core: 2. Of those that a mesh axis runs over, the one named last changes fastest.
Arguments:
- fronts: float32 [8, 4, 8, 2, 128, 128], P('depth', 'tile'), may hold values from -6 to 6
- probe_wave: float32 [2, 128, 128], replicated, may hold values from -6 to 6
- object_slices: bfloat16 [16, 2, 1536, 384], P('depth', None, 'tile')
- patch_list: int32 [11, 4, 3, 8], P(None, 'tile'), may hold values from 0 to 256, as said below
- counts: int32 [11, 4], P(None, 'tile'), may hold values from 1 to 8, as said below
Outputs:
- exit_waves: float32 [8, 4, 8, 2, 128, 128], P('depth', 'tile')
Inputs may be any that keep to these rules, and one draw needn't show every extreme that they name: `patch_list`: rows and columns of corners run from 0 to 256, and that end is reached. Among the live probes of one batch of one owner no tile is named more than 2 times; a batch of 8 probes names every tile exactly 2 times. `counts`: some batch of some owner holds 8 probes.
All inputs are finite; a program needn't handle non-finite values.
Results may differ from a plain program's by a relative error of at most 0.0003.
Values may be sent and summed in bfloat16 or wider, within the bound.
No kernel may reach another device: no remote copies, remote signals or barrier semaphores. Data moves between devices by JAX's collectives and lax.ppermute only.
A program may use at most 64 MiB of HBM per device.

v0:
```python
import functools
import math

import jax
import jax.numpy as jnp
import ml_dtypes
import numpy as np
from jax import lax
from jax.experimental import pallas as pl
from jax.experimental.pallas import tpu as pltpu
from jax.sharding import PartitionSpec as P


STEPS = 4
FRESNEL_RATE = 0.3
EXTRA = 16
PLACES = 4
SPAN = 16
GROUP = 4

HBM = pl.BlockSpec(memory_space=pltpu.MemorySpace.HBM)
VMEM = pl.BlockSpec(memory_space=pltpu.VMEM)
PARAMS = pltpu.CompilerParams(vmem_limit_bytes=24 * 2**20)
SMEM = pl.BlockSpec(memory_space=pltpu.SMEM)


def halves(table):
    high = table.astype(ml_dtypes.bfloat16)
    low = (table - high.astype(np.float64)).astype(ml_dtypes.bfloat16)
    return high, low


@functools.lru_cache(None)
def propagators(width):
    index = np.arange(width)
    angle = 2.0 * np.pi * ((index[:, None] * index[None, :]) % width) / width
    freq = np.where(index < width // 2, index, index - width).astype(np.float64)
    factor = np.exp(-2j * np.pi * FRESNEL_RATE / width * freq**2)
    step = (np.exp(1j * angle) / width) @ (factor[:, None] * np.exp(-1j * angle))
    right = np.block([[step.real, step.imag], [-step.imag, step.real]])
    right_high, right_low = halves(right)
    left_high, left_low = halves(right.T)
    right3 = np.concatenate([right_high, right_high, right_low], axis=0)
    left3 = np.concatenate([left_high, left_high, left_low], axis=1)
    return right3, left3


def split(value):
    high = value.astype(jnp.bfloat16)
    low = (value - high.astype(jnp.float32)).astype(jnp.bfloat16)
    return high, low


def encode(real, imag, store):
    width = real.shape[0]
    codes = []
    for plane, value in enumerate((real, imag)):
        top = jnp.maximum(jnp.max(jnp.abs(value), axis=0, keepdims=True), 2.0**-100)
        code = jnp.ceil((jnp.log(top * (1.0 / 32766.0)) * (256.0 / math.log(2.0))))
        store(plane * width, jnp.round(value * jnp.exp2(code * (-1.0 / 256.0))).astype(jnp.int32).astype(jnp.int16))
        codes.append(code)
    return codes


def extra_rows(codes, places):
    width = codes[0].shape[1]
    rows = [
        jnp.broadcast_to(codes[0], (PLACES, width)),
        jnp.broadcast_to(places, (EXTRA // 2 - PLACES, width)),
        jnp.broadcast_to(codes[1], (EXTRA // 2, width)),
    ]
    return jnp.concatenate(rows, axis=0).astype(jnp.int32).astype(jnp.int16)


def decode(load, width):
    scales = jnp.exp2(load(2 * width, EXTRA).astype(jnp.int32).astype(jnp.float32) * (1.0 / 256.0))
    real = load(0, width).astype(jnp.int32).astype(jnp.float32) * scales[0:1]
    imag = load(width, width).astype(jnp.int32).astype(jnp.float32) * scales[EXTRA // 2 : EXTRA // 2 + 1]
    return real, imag


def nth_of_tile(tile_of, count, slots, tile, nth):
    found = jnp.int32(-1)
    seen = jnp.int32(0)
    for p in range(slots):
        hit = (tile_of(p) == tile) & (p < count)
        found = jnp.where(hit & (seen == nth), p, found)
        seen = seen + hit.astype(jnp.int32)
    return found


def batches():
    depth, depths = lax.axis_index("depth"), lax.axis_size("depth")
    return depths + STEPS - 2 - lax.rem(depth + STEPS - 1, depths), depths + STEPS - 2 - depth


def pack_kernel(tiles, pair, list_ref, count_ref, fronts_ref, slab_ref, right_ref, left_ref, *refs):
    out_refs = refs[:tiles]
    kept_refs = refs[tiles : tiles + 3]
    front_ref, in_sems, keep_sems = refs[tiles + 3 :]
    slots, _, width, _ = fronts_ref.shape
    own = lax.axis_index("tile")
    starting = batches()[0]

    def fetch(p):
        return pltpu.make_async_copy(fronts_ref.at[p], front_ref.at[p], in_sems.at[p])

    keeps = [
        pltpu.make_async_copy(source, target, keep_sems.at[n])
        for n, (source, target) in enumerate(zip((slab_ref, right_ref, left_ref), kept_refs))
    ]
    for p in range(slots):
        pl.when(p < count_ref[0, starting])(lambda p=p: fetch(p).start())
    for copy in keeps:
        copy.start()
    chosen = {}
    for k in range(tiles):
        tile = lax.rem(own + k, tiles)
        for i in range(pair):
            for b, batch in enumerate(batches()):
                chosen[k, i, b] = nth_of_tile(
                    lambda p: list_ref[0, 0, p, batch], count_ref[0, batch], slots, tile, i
                )
    for p in range(slots):
        pl.when(p < count_ref[0, starting])(lambda p=p: fetch(p).wait())
    lane = lax.broadcasted_iota(jnp.int32, (1, width), 1)
    for k in list(range(1, tiles)) + [0]:
        for i in range(pair):
            places = jnp.zeros((1, width), jnp.int32)
            for b, batch in enumerate(batches()):
                p = chosen[k, i, b]
                live = (p >= 0).astype(jnp.int32)
                at = jnp.maximum(p, 0)
                values = (live, list_ref[0, 1, at, batch], list_ref[0, 2, at, batch])
                for offset, value in enumerate(values):
                    places = jnp.where(lane == 3 * b + offset, value, places)
            places = places.astype(jnp.float32)
            p = chosen[k, i, 0]

            def store(row, block):
                out_refs[k][i, row : row + block.shape[0], :] = block

            @pl.when(p >= 0)
            def _():
                store(2 * width, extra_rows(encode(front_ref[p, 0], front_ref[p, 1], store), places))

            @pl.when(p < 0)
            def _():
                none = jnp.zeros((1, width), jnp.float32)
                store(2 * width, extra_rows((none, none), places))

    for copy in keeps:
        copy.wait()


def unpack_kernel(tiles, pair, list_ref, count_ref, *refs):
    in_refs, out_ref = refs[:tiles], refs[tiles]
    exit_ref, out_sems = refs[tiles + 1 :]
    slots, _, width, _ = out_ref.shape
    own = lax.axis_index("tile")
    batch = batches()[1]
    count = count_ref[0, batch]

    def send(p):
        return pltpu.make_async_copy(exit_ref.at[p], out_ref.at[p], out_sems.at[p])

    for p in range(slots):

        @pl.when(p >= count)
        def _():
            exit_ref[p] = jnp.zeros(exit_ref.shape[1:], jnp.float32)
            send(p).start()

    for k in range(tiles):
        tile = lax.rem(own + k, tiles)
        for i in range(pair):
            p = nth_of_tile(lambda p: list_ref[0, 0, p, batch], count, slots, tile, i)

            @pl.when(p >= 0)
            def _():
                real, imag = decode(lambda row, size: in_refs[k][i, row : row + size, :], width)
                exit_ref[p, 0] = real
                exit_ref[p, 1] = imag
                send(p).start()

    for p in range(slots):
        send(p).wait()


def cut(slab_ref, layer, row, column, patch_ref):
    width, side = patch_ref.shape[-1], slab_ref.shape[-1]
    block = jnp.minimum(column // width, side // width - 2)
    shift = column - block * width
    start = pl.multiple_of(row - row_offset(row, width, side), SPAN)
    rows = width + SPAN
    lane = lax.broadcasted_iota(jnp.int32, (rows, width), 1)
    turn = lax.rem(width - shift, width)
    for plane in range(2):
        parts = []
        for b in range(2):
            lanes = pl.ds(pl.multiple_of((block + b) * width, width), width)
            part = pltpu.roll(slab_ref[layer, plane, pl.ds(start, rows), lanes], turn, 1)
            parts.append(part.astype(jnp.float32))
        patch_ref[plane] = jnp.where(lane < width - shift, parts[0], parts[1])


def row_offset(row, width, side):
    return row - jnp.minimum((row // SPAN) * SPAN, side - width - SPAN)


def run_layers(steps, places, wave_ref, patch_ref, x_ref, y_ref, right_ref, left_ref):
    width = wave_ref.shape[1] // 2
    side = steps[0][0].shape[-1]

    def fill(which, turn):
        slab_ref, layer, _ = steps[which]
        for w in range(GROUP):
            cut(slab_ref, layer, *places[w], patch_ref.at[turn, w])

    def one(which):
        turn = which % 2
        for w in range(GROUP):
            rows = slice(w * width, (w + 1) * width)
            part = pl.ds(row_offset(places[w][0], width, side), width)
            real, imag = wave_ref[rows, :width], wave_ref[rows, width:]
            trans_real, trans_imag = patch_ref[turn, w, 0, part, :], patch_ref[turn, w, 1, part, :]
            for plane, value in enumerate((real * trans_real - imag * trans_imag, real * trans_imag + imag * trans_real)):
                high, low = split(value)
                x_ref[rows, plane * width : (plane + 1) * width] = high
                x_ref[rows, (2 + plane) * width : (3 + plane) * width] = low
                x_ref[rows, (4 + plane) * width : (5 + plane) * width] = high
        if which + 1 < len(steps):
            fill(which + 1, 1 - turn)
        spread = jnp.dot(x_ref[...], right_ref[...], preferred_element_type=jnp.float32)
        for w in range(GROUP):
            side_lanes = slice((w % 2) * width, (w % 2 + 1) * width)
            for plane in range(2):
                high, low = split(spread[w * width : (w + 1) * width, plane * width : (plane + 1) * width])
                y_ref[w // 2, plane * width : (plane + 1) * width, side_lanes] = high
                y_ref[w // 2, (2 + plane) * width : (3 + plane) * width, side_lanes] = low
                y_ref[w // 2, (4 + plane) * width : (5 + plane) * width, side_lanes] = high
        for g in range(GROUP // 2):
            out = jnp.dot(left_ref[...], y_ref[g], preferred_element_type=jnp.float32)
            for w in range(2):
                rows = slice((2 * g + w) * width, (2 * g + w + 1) * width)
                side_lanes = slice(w * width, (w + 1) * width)
                wave_ref[rows, :width] = out[:width, side_lanes]
                wave_ref[rows, width:] = out[width:, side_lanes]

    which = 0
    while which < len(steps):
        condition = steps[which][2]
        block = [which]
        while block[-1] + 1 < len(steps) and steps[block[-1] + 1][2] is condition:
            block.append(block[-1] + 1)

        def run(block=tuple(block)):
            if block[0] == 0:
                fill(0, 0)
            for step in block:
                one(step)

        if condition is None:
            run()
        else:
            pl.when(condition)(run)
            later = block[-1] + 1
            if later < len(steps):
                pl.when(jnp.logical_not(condition))(lambda later=later: fill(later, later % 2))
        which = block[-1] + 1


def read_places(in_refs, b, pair, column_ref, place_ref, sem):
    for n, ref in enumerate(in_refs):
        for i in range(pair):
            rows = ref[i, ref.shape[1] - EXTRA :, :].astype(jnp.int32)
            column_ref[n * pair + i : n * pair + i + 1, :] = rows[PLACES : PLACES + 1]
    copy = pltpu.make_async_copy(column_ref, place_ref, sem)
    copy.start()
    copy.wait()
    live, places = [], []
    for j in range(len(in_refs) * pair):
        on = place_ref[j, 3 * b]
        live.append(on == 1)
        places.append((place_ref[j, 3 * b + 1] * on, place_ref[j, 3 * b + 2] * on))
    return live, places


def wave_to(ref, j, width, real, imag):
    rows = slice(j * width, (j + 1) * width)
    ref[rows, :width] = real
    ref[rows, width:] = imag


def send_wave(wave_ref, j, width, ref, at):
    rows = slice(j * width, (j + 1) * width)

    def store(row, block):
        ref[at, row : row + block.shape[0], :] = block

    codes = encode(wave_ref[rows, :width], wave_ref[rows, width:], store)
    store(2 * width, extra_rows(codes, jnp.zeros((1, width), jnp.float32)))


def first_kernel(ks, pair, own_ref, next_ref, probe_ref, right_ref, left_ref, *refs):
    in_refs, move_ref = refs[: len(ks)], refs[len(ks)]
    column_ref, place_ref, sem, wave_ref, patch_ref, x_ref, y_ref = refs[len(ks) + 1 :]
    width = right_ref.shape[1] // 2
    depth, depths = lax.axis_index("depth"), lax.axis_size("depth")
    fresh = depth == depths - 1
    live, places = read_places(in_refs, 0, pair, column_ref, place_ref, sem)
    some = functools.reduce(jnp.logical_or, live)

    @pl.when(some & jnp.logical_or(fresh, depth + STEPS - 1 < depths))
    def _():
        for j in range(GROUP):
            source = in_refs[j // pair]

            @pl.when(fresh)
            def _():
                wave_to(wave_ref, j, width, probe_ref[0], probe_ref[1])

            @pl.when(jnp.logical_not(fresh))
            def _():
                wave_to(wave_ref, j, width, *decode(lambda row, size: source[j % pair, row : row + size, :], width))

        own = jnp.logical_not(fresh)
        steps = [(own_ref, 0, own), (own_ref, 1, own), (next_ref, 0, None), (next_ref, 1, None)]
        run_layers(steps, places, wave_ref, patch_ref, x_ref, y_ref, right_ref, left_ref)
        for j in range(GROUP):
            pl.when(live[j])(lambda j=j: send_wave(wave_ref, j, width, move_ref, j))


def second_kernel(ks, pair, last_ref, own_ref, probe_ref, right_ref, left_ref, arrived_ref, *refs):
    in_refs, out_refs = refs[: len(ks)], refs[len(ks) : 2 * len(ks)]
    column_ref, place_ref, sem, wave_ref, patch_ref, x_ref, y_ref = refs[2 * len(ks) :]
    width = right_ref.shape[1] // 2
    depth = lax.axis_index("depth")
    live, places = read_places(in_refs, 1, pair, column_ref, place_ref, sem)
    some = functools.reduce(jnp.logical_or, live)

    @pl.when(some)
    def _():
        fresh = depth < STEPS - 2
        for j in range(GROUP):

            @pl.when(fresh)
            def _():
                wave_to(wave_ref, j, width, probe_ref[0], probe_ref[1])

            @pl.when(jnp.logical_not(fresh))
            def _():
                wave_to(wave_ref, j, width, *decode(lambda row, size: arrived_ref[j, row : row + size, :], width))

        near = depth >= 1
        steps = [(last_ref, 0, near), (last_ref, 1, near), (own_ref, 0, None), (own_ref, 1, None)]
        run_layers(steps, places, wave_ref, patch_ref, x_ref, y_ref, right_ref, left_ref)
        for j in range(GROUP):
            pl.when(live[j])(lambda j=j: send_wave(wave_ref, j, width, out_refs[j // pair], j % pair))


def on_chip(value):
    return pltpu.with_memory_space_constraint(value, pltpu.MemorySpace.VMEM)


def off_chip(value):
    return pltpu.with_memory_space_constraint(value, pltpu.MemorySpace.HBM)


def per_device(fronts, probe_wave, object_slices, patch_list, counts):
    depths = lax.axis_size("depth")
    tiles = lax.axis_size("tile")
    slots = fronts.shape[2]
    width = fronts.shape[-1]
    pair = slots // tiles
    per_group = GROUP // pair
    groups = [tuple(range(g, g + per_group)) for g in range(0, tiles, per_group)]
    right3, left3 = (jnp.asarray(table) for table in propagators(width))
    coded_rows = 2 * width + EXTRA
    coded = pltpu.VMEM((pair, coded_rows, width), jnp.int16)
    lists = [jnp.transpose(patch_list, (1, 2, 3, 0)), jnp.transpose(counts)]
    lists = [off_chip(value) for value in lists]

    next_slab = on_chip(lax.ppermute(object_slices, "depth", [((d + 1) % depths, d) for d in range(depths)]))
    last_slab = on_chip(lax.ppermute(object_slices, "depth", [(d, d + 1) for d in range(depths - 1)]))
    *packed, own_slab, right, left = pl.pallas_call(
        functools.partial(pack_kernel, tiles, pair),
        out_shape=[coded] * tiles + [pltpu.VMEM(value.shape, value.dtype) for value in (object_slices, right3, left3)],
        in_specs=[SMEM, SMEM, HBM, HBM, HBM, HBM],
        out_specs=[VMEM] * (tiles + 3),
        scratch_shapes=[
            pltpu.VMEM(fronts.shape[2:], jnp.float32),
            pltpu.SemaphoreType.DMA((slots,)),
            pltpu.SemaphoreType.DMA((3,)),
        ],
        compiler_params=PARAMS,
        name="pack",
    )(*lists, *[off_chip(value) for value in (fronts[0, 0], object_slices, right3, left3)])

    def turned(k):
        return [(t, (t + k) % tiles) for t in range(tiles)]

    brought = [packed[0]]
    for k in range(1, tiles):
        brought.append(on_chip(lax.ppermute(packed[k], "tile", turned(k))))
    scratch = [
        pltpu.VMEM((8, width), jnp.int32),
        pltpu.SMEM((8, width), jnp.int32),
        pltpu.SemaphoreType.DMA,
        pltpu.VMEM((GROUP * width, 2 * width), jnp.float32),
        pltpu.VMEM((2, GROUP, 2, width + SPAN, width), jnp.float32),
        pltpu.VMEM((GROUP * width, 6 * width), jnp.bfloat16),
        pltpu.VMEM((GROUP // 2, 6 * width, 2 * width), jnp.bfloat16),
    ]
    moved_shape = pltpu.VMEM((GROUP, coded_rows, width), jnp.int16)
    flops = 2 * GROUP * (2 * 3) * width * (2 * width) ** 2
    arrived = []
    for ks in groups:
        moved = pl.pallas_call(
            functools.partial(first_kernel, ks, pair),
            out_shape=moved_shape,
            in_specs=[VMEM] * (5 + per_group),
            out_specs=VMEM,
            scratch_shapes=scratch,
            cost_estimate=pl.CostEstimate(flops=4 * flops, bytes_accessed=0, transcendentals=0),
            compiler_params=PARAMS,
        )(own_slab, next_slab, probe_wave, right, left, *[brought[k] for k in ks])
        pairs = [(d, d + STEPS - 1) for d in range(depths - STEPS + 1)] + [(depths - 1, STEPS - 2)]
        arrived.append(on_chip(lax.ppermute(moved, "depth", pairs)))
    back = [None] * tiles
    for g, ks in enumerate(groups):
        outs = pl.pallas_call(
            functools.partial(second_kernel, ks, pair),
            out_shape=[coded] * per_group,
            in_specs=[VMEM] * (6 + per_group),
            out_specs=[VMEM] * per_group,
            scratch_shapes=scratch,
            cost_estimate=pl.CostEstimate(flops=4 * flops, bytes_accessed=0, transcendentals=0),
            compiler_params=PARAMS,
        )(last_slab, own_slab, probe_wave, right, left, arrived[g], *[brought[k] for k in ks])
        for k, value in zip(ks, outs):
            if k == 0:
                back[k] = value
            else:
                back[k] = on_chip(lax.ppermute(value, "tile", turned(-k)))
    exits = pl.pallas_call(
        functools.partial(unpack_kernel, tiles, pair),
        out_shape=jax.ShapeDtypeStruct(fronts.shape[2:], jnp.float32),
        in_specs=[SMEM, SMEM] + [VMEM] * tiles,
        out_specs=HBM,
        scratch_shapes=[pltpu.VMEM(fronts.shape[2:], jnp.float32), pltpu.SemaphoreType.DMA((slots,))],
        compiler_params=PARAMS,
        name="unpack",
    )(*lists, *back)
    return exits[None, None]


def solution(mesh):
    in_specs = (
        P("depth", "tile", None, None, None, None),
        P(),
        P("depth", None, "tile", None),
        P(None, "tile", None, None),
        P(None, "tile"),
    )
    out_specs = P("depth", "tile", None, None, None, None)

    return jax.shard_map(per_device, mesh=mesh, in_specs=in_specs, out_specs=out_specs, check_vma=False)
```

profile of v0, /device:TPU:1, one launch (start us, length us, event | category | flops | bytes accessed | tf_op | source)
XLA Modules:
  0.0 67.1 jit_solution(1891578633593974378)
XLA Ops:
  0.0 0.0 collective-permute-start.1
  0.0 4.5 %collective-permute-start = (bf16[2,2,384,384]{3,2,1,0:T(8,128)(2,1)}, bf16[2,2,384,384]{3,2,1,0:T(8,128)(2,1)S(1)}, u32[]{:S(2)}, u32[]{:S(2)}) collective-permute-start(bf16[2,2,384,384]{3,2,1,0:T(8,128)(2,1)} %slab_ref.1), channel_id=1, source_target_pairs={{0,4},{4,8},{8,12},{12,16},{16,20},{20,24},{24,28},{1,5},{5,9},{9,... | collective-permute-start | bytes 3538952 | tf_op jit(solution)/shard_map/ppermute | solution.py:385
  4.5 0.0 copy-start
  4.5 3.1 %pack.1 = (s16[2,272,128]{2,1,0:T(8,128)(2,1)S(1)}, s16[2,272,128]{2,1,0:T(8,128)(2,1)S(1)}, s16[2,272,128]{2,1,0:T(8,128)(2,1)S(1)}, s16[2,272,128]{2,1,0:T(8,1...) custom-call(s32[1,3,8,11]{3,2,1,0:T(8,128)} %bitcast.5, ...), custom_call_target="tpu_custom_call" | custom-call | tf_op jit(solution)/shard_map/pack/pallas_call | solution.py:386
  7.7 1.2 %collective-permute-start.2 = (s16[2,272,128]{2,1,0:T(8,128)(2,1)S(1)}, s16[2,272,128]{2,1,0:T(8,128)(2,1)S(1)}, u32[]{:S(2)}, u32[]{:S(2)}) collective-permute-start(s16[2,272,128]{2,1,0:T(8,128)(2,1)S(1)} %get-tuple-element.20), channel_id=1, source_target_pairs={{0,1},{1,2},{2,3},{3,0},{4,5},{5,6},{6,7},{7,4},{8,9},{9,10},{10,1... | collective-permute-start | bytes 417800 | tf_op jit(solution)/shard_map/ppermute | solution.py:405
  8.9 2.4 %collective-permute-start.5 = (s16[2,272,128]{2,1,0:T(8,128)(2,1)S(1)}, s16[2,272,128]{2,1,0:T(8,128)(2,1)S(1)}, u32[]{:S(2)}, u32[]{:S(2)}) collective-permute-start(s16[2,272,128]{2,1,0:T(8,128)(2,1)S(1)} %get-tuple-element.23), channel_id=1, source_target_pairs={{0,2},{1,3},{2,0},{3,1},{4,6},{5,7},{6,4},{7,5},{8,10},{9,11},{10,... | collective-permute-start | bytes 417800 | tf_op jit(solution)/shard_map/ppermute | solution.py:405
  11.3 0.9 %collective-permute-start.6 = (s16[2,272,128]{2,1,0:T(8,128)(2,1)S(1)}, s16[2,272,128]{2,1,0:T(8,128)(2,1)S(1)}, u32[]{:S(2)}, u32[]{:S(2)}) collective-permute-start(s16[2,272,128]{2,1,0:T(8,128)(2,1)S(1)} %get-tuple-element.24), channel_id=1, source_target_pairs={{0,3},{1,0},{2,1},{3,2},{4,7},{5,4},{6,5},{7,6},{8,11},{9,8},{10,9... | collective-permute-start | bytes 417800 | tf_op jit(solution)/shard_map/ppermute | solution.py:405
  12.2 2.6 %collective-permute-done.2.refs_1_ = s16[2,272,128]{2,1,0:T(8,128)(2,1)S(1)} collective-permute-done((s16[2,272,128]{2,1,0:T(8,128)(2,1)S(1)}, s16[2,272,128]{2,1,0:T(8,128)(2,1)S(1)}, u32[]{:S(2)}, u32[]{:S(2)}) %collective-permute-start.2) | collective-permute-done | bytes 139296 | tf_op jit(solution)/shard_map/ppermute | solution.py:405
  14.8 10.8 %collective-permute-done.1.next_ref = bf16[2,2,384,384]{3,2,1,0:T(8,128)(2,1)S(1)} collective-permute-done((bf16[2,2,384,384]{3,2,1,0:T(8,128)(2,1)}, bf16[2,2,384,384]{3,2,1,0:T(8,128)(2,1)S(1)}, u32[]{:S(2)}, u32[]{:S(2)}) %collective-permute-start.1) | collective-permute-done | bytes 1179680 | tf_op jit(solution)/shard_map/ppermute | solution.py:384
  25.7 0.0 copy-done
  25.7 0.6 shard_map.73
  26.3 9.0 %collective-permute-start.3 = (s16[4,272,128]{2,1,0:T(8,128)(2,1)S(1)}, s16[4,272,128]{2,1,0:T(8,128)(2,1)S(1)}, u32[]{:S(2)}, u32[]{:S(2)}) collective-permute-start(s16[4,272,128]{2,1,0:T(8,128)(2,1)S(1)} %shard_map.73), channel_id=1, source_target_pairs={{0,12},{4,16},{8,20},{12,24},{16,28},{28,8},{1,13},{5,17},{9,21},{... | collective-permute-start | bytes 835592 | tf_op jit(solution)/shard_map/ppermute | solution.py:429
  35.3 0.0 collective-permute-done.5.refs_0_
  35.3 0.0 collective-permute-done.6.refs_1_
  35.3 5.1 %shard_map.75 = s16[4,272,128]{2,1,0:T(8,128)(2,1)S(1)} custom-call(bf16[2,2,384,384]{3,2,1,0:T(8,128)(2,1)S(1)} %get-tuple-element.16.own_ref, bf16[2,2,384,384]{3,2,1,0:T(8,128)(2,1)S(1)} %collective-permute-done.1.next_ref, f32[2,128,128]{2,1,0:T(8,128)S(1)} %copy-done, bf16[768,256]{1,0:T(8,128)(2,1)S(1)} %get-tuple-element.17.right_ref, ...), custom_call_target="tpu_custom_call" | custom-call | flops 1610612736 | tf_op jit(solution)/shard_map/pallas_call | solution.py:419
  40.5 1.3 %collective-permute-start.7 = (s16[4,272,128]{2,1,0:T(8,128)(2,1)S(1)}, s16[4,272,128]{2,1,0:T(8,128)(2,1)S(1)}, u32[]{:S(2)}, u32[]{:S(2)}) collective-permute-start(s16[4,272,128]{2,1,0:T(8,128)(2,1)S(1)} %shard_map.75), channel_id=1, source_target_pairs={{0,12},{4,16},{8,20},{12,24},{16,28},{28,8},{1,13},{5,17},{9,21},{... | collective-permute-start | bytes 835592 | tf_op jit(solution)/shard_map/ppermute | solution.py:429
  41.8 0.0 collective-permute-done.last_ref
  41.8 0.0 collective-permute-done.3.arrived_ref
  41.8 5.3 %shard_map.74 = (s16[2,272,128]{2,1,0:T(8,128)(2,1)S(1)}, s16[2,272,128]{2,1,0:T(8,128)(2,1)S(1)}) custom-call(bf16[2,2,384,384]{3,2,1,0:T(8,128)(2,1)S(1)} %collective-permute-done.last_ref, bf16[2,2,384,384]{3,2,1,0:T(8,128)(2,1)S(1)} %get-tuple-element.16.own_ref, f32[2,128,128]{2,1,0:T(8,128)S(1)} %copy-done, ...), custom_call_target="tpu_custom_call" | custom-call | flops 1610612736 | tf_op jit(solution)/shard_map/pallas_call | solution.py:432
  47.1 5.7 %collective-permute-start.4 = (s16[2,272,128]{2,1,0:T(8,128)(2,1)S(1)}, s16[2,272,128]{2,1,0:T(8,128)(2,1)S(1)}, u32[]{:S(2)}, u32[]{:S(2)}) collective-permute-start(s16[2,272,128]{2,1,0:T(8,128)(2,1)S(1)} %get-tuple-element.22), channel_id=1, source_target_pairs={{0,3},{1,0},{2,1},{3,2},{4,7},{5,4},{6,5},{7,6},{8,11},{9,8},{10,9... | collective-permute-start | bytes 417800 | tf_op jit(solution)/shard_map/ppermute | solution.py:445
  52.8 0.0 collective-permute-done.7.arrived_ref
  52.8 5.2 %shard_map.76 = (s16[2,272,128]{2,1,0:T(8,128)(2,1)S(1)}, s16[2,272,128]{2,1,0:T(8,128)(2,1)S(1)}) custom-call(bf16[2,2,384,384]{3,2,1,0:T(8,128)(2,1)S(1)} %collective-permute-done.last_ref, bf16[2,2,384,384]{3,2,1,0:T(8,128)(2,1)S(1)} %get-tuple-element.16.own_ref, f32[2,128,128]{2,1,0:T(8,128)S(1)} %copy-done, ...), custom_call_target="tpu_custom_call" | custom-call | flops 1610612736 | tf_op jit(solution)/shard_map/pallas_call | solution.py:432
  58.0 0.1 collective-permute-start.8
  58.0 0.1 collective-permute-start.9
  58.1 0.0 collective-permute-done.4.refs_1_
  58.1 6.8 %collective-permute-done.8.refs_2_ = s16[2,272,128]{2,1,0:T(8,128)(2,1)S(1)} collective-permute-done((s16[2,272,128]{2,1,0:T(8,128)(2,1)S(1)}, s16[2,272,128]{2,1,0:T(8,128)(2,1)S(1)}, u32[]{:S(2)}, u32[]{:S(2)}) %collective-permute-start.8) | collective-permute-done | bytes 139296 | tf_op jit(solution)/shard_map/ppermute | solution.py:445
  65.0 0.0 collective-permute-done.9.refs_3_
  65.0 1.9 %unpack.1 = f32[8,2,128,128]{3,2,1,0:T(8,128)} custom-call(s32[1,3,8,11]{3,2,1,0:T(8,128)} %bitcast.6, s32[1,11]{1,0:T(1,128)} %bitcast.8, s16[2,272,128]{2,1,0:T(8,128)(2,1)S(1)} %get-tuple-element.21.refs_0_, s16[2,272,128]{2,1,0:T(8,128)(2,1)S(1)} %collective-permute-done.4.refs_1_, s16[2,272,128]{2,1,0:T(8,128)(2,1)S(1)} %collective-permute-done.8.refs_2_, ...), custom_call_target="tpu_custom_call" | custom-call | tf_op jit(solution)/shard_map/unpack/pallas_call | solution.py:446
Async XLA Ops:
  0.0 25.7 %collective-permute-start.1 = (bf16[2,2,384,384]{3,2,1,0:T(8,128)(2,1)}, bf16[2,2,384,384]{3,2,1,0:T(8,128)(2,1)S(1)}, u32[]{:S(2)}, u32[]{:S(2)}) collective-permute-start(bf16[2,2,384,384]{3,2,1,0:T(8,128)(2,1)} %slab_ref.1), channel_id=1, source_target_pairs={{4,0},{8,4},{12,8},{16,12},{20,16},{24,20},{28,24},{0,28},{5,1},{9... | collective-permute-start | bytes 3538952 | tf_op jit(solution)/shard_map/ppermute | solution.py:384
  0.0 41.8 %collective-permute-start = (bf16[2,2,384,384]{3,2,1,0:T(8,128)(2,1)}, bf16[2,2,384,384]{3,2,1,0:T(8,128)(2,1)S(1)}, u32[]{:S(2)}, u32[]{:S(2)}) collective-permute-start(bf16[2,2,384,384]{3,2,1,0:T(8,128)(2,1)} %slab_ref.1), channel_id=1, source_target_pairs={{0,4},{4,8},{8,12},{12,16},{16,20},{20,24},{24,28},{1,5},{5,9},{9,... | collective-permute-start | bytes 3538952 | tf_op jit(solution)/shard_map/ppermute | solution.py:385
  4.5 21.2 %copy-start = (f32[2,128,128]{2,1,0:T(8,128)S(1)}, f32[2,128,128]{2,1,0:T(8,128)}, u32[]{:S(2)}) copy-start(f32[2,128,128]{2,1,0:T(8,128)} %probe_ref.7) | copy-start | bytes 393220
  7.7 7.2 %collective-permute-start.2 = (s16[2,272,128]{2,1,0:T(8,128)(2,1)S(1)}, s16[2,272,128]{2,1,0:T(8,128)(2,1)S(1)}, u32[]{:S(2)}, u32[]{:S(2)}) collective-permute-start(s16[2,272,128]{2,1,0:T(8,128)(2,1)S(1)} %get-tuple-element.20), channel_id=1, source_target_pairs={{0,1},{1,2},{2,3},{3,0},{4,5},{5,6},{6,7},{7,4},{8,9},{9,10},{10,1... | collective-permute-start | bytes 417800 | tf_op jit(solution)/shard_map/ppermute | solution.py:405
  8.9 26.4 %collective-permute-start.5 = (s16[2,272,128]{2,1,0:T(8,128)(2,1)S(1)}, s16[2,272,128]{2,1,0:T(8,128)(2,1)S(1)}, u32[]{:S(2)}, u32[]{:S(2)}) collective-permute-start(s16[2,272,128]{2,1,0:T(8,128)(2,1)S(1)} %get-tuple-element.23), channel_id=1, source_target_pairs={{0,2},{1,3},{2,0},{3,1},{4,6},{5,7},{6,4},{7,5},{8,10},{9,11},{10,... | collective-permute-start | bytes 417800 | tf_op jit(solution)/shard_map/ppermute | solution.py:405
  11.3 24.0 %collective-permute-start.6 = (s16[2,272,128]{2,1,0:T(8,128)(2,1)S(1)}, s16[2,272,128]{2,1,0:T(8,128)(2,1)S(1)}, u32[]{:S(2)}, u32[]{:S(2)}) collective-permute-start(s16[2,272,128]{2,1,0:T(8,128)(2,1)S(1)} %get-tuple-element.24), channel_id=1, source_target_pairs={{0,3},{1,0},{2,1},{3,2},{4,7},{5,4},{6,5},{7,6},{8,11},{9,8},{10,9... | collective-permute-start | bytes 417800 | tf_op jit(solution)/shard_map/ppermute | solution.py:405
  26.3 15.5 %collective-permute-start.3 = (s16[4,272,128]{2,1,0:T(8,128)(2,1)S(1)}, s16[4,272,128]{2,1,0:T(8,128)(2,1)S(1)}, u32[]{:S(2)}, u32[]{:S(2)}) collective-permute-start(s16[4,272,128]{2,1,0:T(8,128)(2,1)S(1)} %shard_map.73), channel_id=1, source_target_pairs={{0,12},{4,16},{8,20},{12,24},{16,28},{28,8},{1,13},{5,17},{9,21},{... | collective-permute-start | bytes 835592 | tf_op jit(solution)/shard_map/ppermute | solution.py:429
  40.5 12.3 %collective-permute-start.7 = (s16[4,272,128]{2,1,0:T(8,128)(2,1)S(1)}, s16[4,272,128]{2,1,0:T(8,128)(2,1)S(1)}, u32[]{:S(2)}, u32[]{:S(2)}) collective-permute-start(s16[4,272,128]{2,1,0:T(8,128)(2,1)S(1)} %shard_map.75), channel_id=1, source_target_pairs={{0,12},{4,16},{8,20},{12,24},{16,28},{28,8},{1,13},{5,17},{9,21},{... | collective-permute-start | bytes 835592 | tf_op jit(solution)/shard_map/ppermute | solution.py:429
  47.1 11.0 %collective-permute-start.4 = (s16[2,272,128]{2,1,0:T(8,128)(2,1)S(1)}, s16[2,272,128]{2,1,0:T(8,128)(2,1)S(1)}, u32[]{:S(2)}, u32[]{:S(2)}) collective-permute-start(s16[2,272,128]{2,1,0:T(8,128)(2,1)S(1)} %get-tuple-element.22), channel_id=1, source_target_pairs={{0,3},{1,0},{2,1},{3,2},{4,7},{5,4},{6,5},{7,6},{8,11},{9,8},{10,9... | collective-permute-start | bytes 417800 | tf_op jit(solution)/shard_map/ppermute | solution.py:445
  58.0 7.0 %collective-permute-start.8 = (s16[2,272,128]{2,1,0:T(8,128)(2,1)S(1)}, s16[2,272,128]{2,1,0:T(8,128)(2,1)S(1)}, u32[]{:S(2)}, u32[]{:S(2)}) collective-permute-start(s16[2,272,128]{2,1,0:T(8,128)(2,1)S(1)} %get-tuple-element.25), channel_id=1, source_target_pairs={{0,2},{1,3},{2,0},{3,1},{4,6},{5,7},{6,4},{7,5},{8,10},{9,11},{10,... | collective-permute-start | bytes 417800 | tf_op jit(solution)/shard_map/ppermute | solution.py:445
  58.0 6.9 %collective-permute-start.9 = (s16[2,272,128]{2,1,0:T(8,128)(2,1)S(1)}, s16[2,272,128]{2,1,0:T(8,128)(2,1)S(1)}, u32[]{:S(2)}, u32[]{:S(2)}) collective-permute-start(s16[2,272,128]{2,1,0:T(8,128)(2,1)S(1)} %get-tuple-element.26), channel_id=1, source_target_pairs={{0,1},{1,2},{2,3},{3,0},{4,5},{5,6},{6,7},{7,4},{8,9},{9,10},{10,1... | collective-permute-start | bytes 417800 | tf_op jit(solution)/shard_map/ppermute | solution.py:445
where the time goes:
time: 67.4 us; the launch traced here: 67.1 us
  starting transfers between devices  25.1 us (37%)
  Pallas kernels  21.4 us (32%)
  waiting for transfers between devices  20.3 us (30%)
    ppermute x1, waiting for transfers between devices, per_device(): lax.ppermute(object_slices, 'depth', [((d + 1) % depths, d) for d in rang...  10.8 us
    pallas_call x2, Pallas kernels, per_device(): pl.pallas_call(functools.partial(second_kernel, ks, pair), out_shape=[cod...  10.5 us
    ppermute x2, starting transfers between devices, per_device(): arrived.append(on_chip(lax.ppermute(moved, 'depth', pairs)))  10.3 us
    ppermute x3, waiting for transfers between devices, per_device(): back[k] = on_chip(lax.ppermute(value, 'tile', turned(-k)))  6.85 us
    ppermute x3, starting transfers between devices, per_device(): back[k] = on_chip(lax.ppermute(value, 'tile', turned(-k)))  5.78 us
    pallas_call x2, Pallas kernels, per_device(): pl.pallas_call(functools.partial(first_kernel, ks, pair), out_shape=moved...  5.77 us
    ppermute x3, starting transfers between devices, per_device(): brought.append(on_chip(lax.ppermute(packed[k], 'tile', turned(k))))  4.56 us
    ppermute x1, starting transfers between devices, per_device(): lax.ppermute(object_slices, 'depth', [(d, d + 1) for d in range(depths -...  4.47 us
  transfers between devices with their start and end apart: 10, of which 3 were waited for; matrix products, arithmetic and copies ran while one was open for 0% of the time, Pallas kernels for 29%

commit v1 on v0

--- a/solution.py
+++ b/solution.py
@@ -94,10 +94,20 @@
     return depths + STEPS - 2 - lax.rem(depth + STEPS - 1, depths), depths + STEPS - 2 - depth
 
 
-def pack_kernel(tiles, pair, list_ref, count_ref, fronts_ref, slab_ref, right_ref, left_ref, *refs):
+def prep_kernel(slab_ref, right_ref, left_ref, probe_ref, *refs):
+    copies = [
+        pltpu.make_async_copy(source, target, refs[4].at[n])
+        for n, (source, target) in enumerate(zip((slab_ref, right_ref, left_ref, probe_ref), refs[:4]))
+    ]
+    for copy in copies:
+        copy.start()
+    for copy in copies:
+        copy.wait()
+
+
+def pack_kernel(tiles, pair, list_ref, count_ref, fronts_ref, *refs):
     out_refs = refs[:tiles]
-    kept_refs = refs[tiles : tiles + 3]
-    front_ref, in_sems, keep_sems = refs[tiles + 3 :]
+    front_ref, in_sems = refs[tiles:]
     slots, _, width, _ = fronts_ref.shape
     own = lax.axis_index("tile")
     starting = batches()[0]
@@ -105,14 +115,8 @@
     def fetch(p):
         return pltpu.make_async_copy(fronts_ref.at[p], front_ref.at[p], in_sems.at[p])
 
-    keeps = [
-        pltpu.make_async_copy(source, target, keep_sems.at[n])
-        for n, (source, target) in enumerate(zip((slab_ref, right_ref, left_ref), kept_refs))
-    ]
     for p in range(slots):
         pl.when(p < count_ref[0, starting])(lambda p=p: fetch(p).start())
-    for copy in keeps:
-        copy.start()
     chosen = {}
     for k in range(tiles):
         tile = lax.rem(own + k, tiles)
@@ -149,9 +153,6 @@
                 none = jnp.zeros((1, width), jnp.float32)
                 store(2 * width, extra_rows((none, none), places))
 
-    for copy in keeps:
-        copy.wait()
-
 
 def unpack_kernel(tiles, pair, list_ref, count_ref, *refs):
     in_refs, out_ref = refs[:tiles], refs[tiles]
@@ -208,44 +209,60 @@
     return row - jnp.minimum((row // SPAN) * SPAN, side - width - SPAN)
 
 
-def run_layers(steps, places, wave_ref, patch_ref, x_ref, y_ref, right_ref, left_ref):
+def run_layers(steps, places, wave_ref, patch_ref, x_refs, y_refs, right_ref, left_ref):
     width = wave_ref.shape[1] // 2
     side = steps[0][0].shape[-1]
 
-    def fill(which, turn):
+    def fill(which, turn, pair):
         slab_ref, layer, _ = steps[which]
-        for w in range(GROUP):
+        for w in (2 * pair, 2 * pair + 1):
             cut(slab_ref, layer, *places[w], patch_ref.at[turn, w])
 
-    def one(which):
+    def multiply(which, pair):
         turn = which % 2
-        for w in range(GROUP):
+        for n in range(2):
+            w = 2 * pair + n
             rows = slice(w * width, (w + 1) * width)
             part = pl.ds(row_offset(places[w][0], width, side), width)
             real, imag = wave_ref[rows, :width], wave_ref[rows, width:]
             trans_real, trans_imag = patch_ref[turn, w, 0, part, :], patch_ref[turn, w, 1, part, :]
+            rows = slice(n * width, (n + 1) * width)
             for plane, value in enumerate((real * trans_real - imag * trans_imag, real * trans_imag + imag * trans_real)):
                 high, low = split(value)
-                x_ref[rows, plane * width : (plane + 1) * width] = high
-                x_ref[rows, (2 + plane) * width : (3 + plane) * width] = low
-                x_ref[rows, (4 + plane) * width : (5 + plane) * width] = high
-        if which + 1 < len(steps):
-            fill(which + 1, 1 - turn)
-        spread = jnp.dot(x_ref[...], right_ref[...], preferred_element_type=jnp.float32)
-        for w in range(GROUP):
-            side_lanes = slice((w % 2) * width, (w % 2 + 1) * width)
+                x_refs[pair][rows, plane * width : (plane + 1) * width] = high
+                x_refs[pair][rows, (2 + plane) * width : (3 + plane) * width] = low
+
+    def right(pair):
+        x = x_refs[pair][...]
+        x = jnp.concatenate([x, x[:, : 2 * width]], axis=1)
+        spread = jnp.dot(x, right_ref[...], preferred_element_type=jnp.float32)
+        for n in range(2):
+            lanes = slice(n * width, (n + 1) * width)
             for plane in range(2):
-                high, low = split(spread[w * width : (w + 1) * width, plane * width : (plane + 1) * width])
-                y_ref[w // 2, plane * width : (plane + 1) * width, side_lanes] = high
-                y_ref[w // 2, (2 + plane) * width : (3 + plane) * width, side_lanes] = low
-                y_ref[w // 2, (4 + plane) * width : (5 + plane) * width, side_lanes] = high
-        for g in range(GROUP // 2):
-            out = jnp.dot(left_ref[...], y_ref[g], preferred_element_type=jnp.float32)
-            for w in range(2):
-                rows = slice((2 * g + w) * width, (2 * g + w + 1) * width)
-                side_lanes = slice(w * width, (w + 1) * width)
-                wave_ref[rows, :width] = out[:width, side_lanes]
-                wave_ref[rows, width:] = out[width:, side_lanes]
+                high, low = split(spread[n * width : (n + 1) * width, plane * width : (plane + 1) * width])
+                y_refs[pair][plane * width : (plane + 1) * width, lanes] = high
+                y_refs[pair][(2 + plane) * width : (3 + plane) * width, lanes] = low
+
+    def left(pair):
+        y = y_refs[pair][...]
+        y = jnp.concatenate([y, y[: 2 * width]], axis=0)
+        out = jnp.dot(left_ref[...], y, preferred_element_type=jnp.float32)
+        for n in range(2):
+            w = 2 * pair + n
+            rows = slice(w * width, (w + 1) * width)
+            lanes = slice(n * width, (n + 1) * width)
+            wave_ref[rows, :width] = out[:width, lanes]
+            wave_ref[rows, width:] = out[width:, lanes]
+
+    def one(which):
+        for pair in range(GROUP // 2):
+            multiply(which, pair)
+        for pair in range(GROUP // 2):
+            right(pair)
+            if which + 1 < len(steps):
+                fill(which + 1, 1 - which % 2, pair)
+        for pair in range(GROUP // 2):
+            left(pair)
 
     which = 0
     while which < len(steps):
@@ -256,7 +273,8 @@
 
         def run(block=tuple(block)):
             if block[0] == 0:
-                fill(0, 0)
+                for pair in range(GROUP // 2):
+                    fill(0, 0, pair)
             for step in block:
                 one(step)
 
@@ -266,7 +284,12 @@
             pl.when(condition)(run)
             later = block[-1] + 1
             if later < len(steps):
-                pl.when(jnp.logical_not(condition))(lambda later=later: fill(later, later % 2))
+
+                def skip(later=later):
+                    for pair in range(GROUP // 2):
+                        fill(later, later % 2, pair)
+
+                pl.when(jnp.logical_not(condition))(skip)
         which = block[-1] + 1
 
 
@@ -304,7 +327,7 @@
 
 def first_kernel(ks, pair, own_ref, next_ref, probe_ref, right_ref, left_ref, *refs):
     in_refs, move_ref = refs[: len(ks)], refs[len(ks)]
-    column_ref, place_ref, sem, wave_ref, patch_ref, x_ref, y_ref = refs[len(ks) + 1 :]
+    column_ref, place_ref, sem, wave_ref, patch_ref, *buffers = refs[len(ks) + 1 :]
     width = right_ref.shape[1] // 2
     depth, depths = lax.axis_index("depth"), lax.axis_size("depth")
     fresh = depth == depths - 1
@@ -326,14 +349,14 @@
 
         own = jnp.logical_not(fresh)
         steps = [(own_ref, 0, own), (own_ref, 1, own), (next_ref, 0, None), (next_ref, 1, None)]
-        run_layers(steps, places, wave_ref, patch_ref, x_ref, y_ref, right_ref, left_ref)
+        run_layers(steps, places, wave_ref, patch_ref, buffers[:2], buffers[2:], right_ref, left_ref)
         for j in range(GROUP):
             pl.when(live[j])(lambda j=j: send_wave(wave_ref, j, width, move_ref, j))
 
 
 def second_kernel(ks, pair, last_ref, own_ref, probe_ref, right_ref, left_ref, arrived_ref, *refs):
     in_refs, out_refs = refs[: len(ks)], refs[len(ks) : 2 * len(ks)]
-    column_ref, place_ref, sem, wave_ref, patch_ref, x_ref, y_ref = refs[2 * len(ks) :]
+    column_ref, place_ref, sem, wave_ref, patch_ref, *buffers = refs[2 * len(ks) :]
     width = right_ref.shape[1] // 2
     depth = lax.axis_index("depth")
     live, places = read_places(in_refs, 1, pair, column_ref, place_ref, sem)
@@ -354,7 +377,7 @@
 
         near = depth >= 1
         steps = [(last_ref, 0, near), (last_ref, 1, near), (own_ref, 0, None), (own_ref, 1, None)]
-        run_layers(steps, places, wave_ref, patch_ref, x_ref, y_ref, right_ref, left_ref)
+        run_layers(steps, places, wave_ref, patch_ref, buffers[:2], buffers[2:], right_ref, left_ref)
         for j in range(GROUP):
             pl.when(live[j])(lambda j=j: send_wave(wave_ref, j, width, out_refs[j // pair], j % pair))
 
@@ -374,7 +397,7 @@
     width = fronts.shape[-1]
     pair = slots // tiles
     per_group = GROUP // pair
-    groups = [tuple(range(g, g + per_group)) for g in range(0, tiles, per_group)]
+    groups = [tuple(range(g, g + per_group)) for g in range(0, tiles, per_group)][::-1]
     right3, left3 = (jnp.asarray(table) for table in propagators(width))
     coded_rows = 2 * width + EXTRA
     coded = pltpu.VMEM((pair, coded_rows, width), jnp.int16)
@@ -383,19 +406,25 @@
 
     next_slab = on_chip(lax.ppermute(object_slices, "depth", [((d + 1) % depths, d) for d in range(depths)]))
     last_slab = on_chip(lax.ppermute(object_slices, "depth", [(d, d + 1) for d in range(depths - 1)]))
-    *packed, own_slab, right, left = pl.pallas_call(
+    packed = pl.pallas_call(
         functools.partial(pack_kernel, tiles, pair),
-        out_shape=[coded] * tiles + [pltpu.VMEM(value.shape, value.dtype) for value in (object_slices, right3, left3)],
-        in_specs=[SMEM, SMEM, HBM, HBM, HBM, HBM],
-        out_specs=[VMEM] * (tiles + 3),
-        scratch_shapes=[
-            pltpu.VMEM(fronts.shape[2:], jnp.float32),
-            pltpu.SemaphoreType.DMA((slots,)),
-            pltpu.SemaphoreType.DMA((3,)),
-        ],
+        out_shape=[coded] * tiles,
+        in_specs=[SMEM, SMEM, HBM],
+        out_specs=[VMEM] * tiles,
+        scratch_shapes=[pltpu.VMEM(fronts.shape[2:], jnp.float32), pltpu.SemaphoreType.DMA((slots,))],
         compiler_params=PARAMS,
         name="pack",
-    )(*lists, *[off_chip(value) for value in (fronts[0, 0], object_slices, right3, left3)])
+    )(*lists, off_chip(fronts[0, 0]))
+    kept = (object_slices, right3, left3, probe_wave)
+    own_slab, right, left, probe = pl.pallas_call(
+        prep_kernel,
+        out_shape=[pltpu.VMEM(value.shape, value.dtype) for value in kept],
+        in_specs=[HBM] * 4,
+        out_specs=[VMEM] * 4,
+        scratch_shapes=[pltpu.SemaphoreType.DMA((4,))],
+        compiler_params=PARAMS,
+        name="prep",
+    )(*[off_chip(value) for value in kept])
 
     def turned(k):
         return [(t, (t + k) % tiles) for t in range(tiles)]
@@ -409,8 +438,8 @@
         pltpu.SemaphoreType.DMA,
         pltpu.VMEM((GROUP * width, 2 * width), jnp.float32),
         pltpu.VMEM((2, GROUP, 2, width + SPAN, width), jnp.float32),
-        pltpu.VMEM((GROUP * width, 6 * width), jnp.bfloat16),
-        pltpu.VMEM((GROUP // 2, 6 * width, 2 * width), jnp.bfloat16),
+        *[pltpu.VMEM((2 * width, 4 * width), jnp.bfloat16)] * (GROUP // 2),
+        *[pltpu.VMEM((4 * width, 2 * width), jnp.bfloat16)] * (GROUP // 2),
     ]
     moved_shape = pltpu.VMEM((GROUP, coded_rows, width), jnp.int16)
     flops = 2 * GROUP * (2 * 3) * width * (2 * width) ** 2
@@ -424,7 +453,7 @@
             scratch_shapes=scratch,
             cost_estimate=pl.CostEstimate(flops=4 * flops, bytes_accessed=0, transcendentals=0),
             compiler_params=PARAMS,
-        )(own_slab, next_slab, probe_wave, right, left, *[brought[k] for k in ks])
+        )(own_slab, next_slab, probe, right, left, *[brought[k] for k in ks])
         pairs = [(d, d + STEPS - 1) for d in range(depths - STEPS + 1)] + [(depths - 1, STEPS - 2)]
         arrived.append(on_chip(lax.ppermute(moved, "depth", pairs)))
     back = [None] * tiles
@@ -437,7 +466,7 @@
             scratch_shapes=scratch,
             cost_estimate=pl.CostEstimate(flops=4 * flops, bytes_accessed=0, transcendentals=0),
             compiler_params=PARAMS,
-        )(last_slab, own_slab, probe_wave, right, left, arrived[g], *[brought[k] for k in ks])
+        )(last_slab, own_slab, probe, right, left, arrived[g], *[brought[k] for k in ks])
         for k, value in zip(ks, outs):
             if k == 0:
                 back[k] = value

time: 67.4 us -> 66.4 us (0.985)
  Pallas kernels: 21.4 us -> 20.4 us
    pallas_call x0 -> x1, Pallas kernels: none -> 1.53 us  [per_device(): pl.pallas_call(prep_kernel, out_shape=[pltpu.VMEM(value.shape, value.dtyp...]
    pallas_call x2, Pallas kernels: 10.5 us -> 9.25 us  [per_device(): pl.pallas_call(functools.partial(second_kernel, ks, pair), out_shape=[cod...]
    ppermute x3, waiting for transfers between devices: 6.85 us -> 7.92 us  [per_device(): back[k] = on_chip(lax.ppermute(value, 'tile', turned(-k)))]
    ppermute x3, waiting for transfers between devices: 2.6 us -> 1.61 us  [per_device(): brought.append(on_chip(lax.ppermute(packed[k], 'tile', turned(k))))]
    pallas_call x2, Pallas kernels: 5.77 us -> 4.99 us  [per_device(): pl.pallas_call(functools.partial(first_kernel, ks, pair), out_shape=moved...]
    ppermute x2, starting transfers between devices: 10.3 us -> 9.53 us  [per_device(): arrived.append(on_chip(lax.ppermute(moved, 'depth', pairs)))]
  transfers between devices with their start and end apart: 10 -> 10, of which waited for: 3 -> 3; matrix products, arithmetic and copies ran while one was open for 0% -> 0% of each run, Pallas kernels for 29% -> 28%
where the time goes in v1:
time: 66.4 us; the launch traced here: 65.7 us
  starting transfers between devices  24.6 us (37%)
  Pallas kernels  20.4 us (31%)
  waiting for transfers between devices  20.4 us (31%)
    ppermute x1, waiting for transfers between devices, per_device(): lax.ppermute(object_slices, 'depth', [((d + 1) % depths, d) for d in rang...  10.9 us
    ppermute x2, starting transfers between devices, per_device(): arrived.append(on_chip(lax.ppermute(moved, 'depth', pairs)))  9.53 us
    pallas_call x2, Pallas kernels, per_device(): pl.pallas_call(functools.partial(second_kernel, ks, pair), out_shape=[cod...  9.25 us
    ppermute x3, waiting for transfers between devices, per_device(): back[k] = on_chip(lax.ppermute(value, 'tile', turned(-k)))  7.92 us
    ppermute x3, starting transfers between devices, per_device(): back[k] = on_chip(lax.ppermute(value, 'tile', turned(-k)))  6.12 us
    pallas_call x2, Pallas kernels, per_device(): pl.pallas_call(functools.partial(first_kernel, ks, pair), out_shape=moved...  4.99 us
    ppermute x1, starting transfers between devices, per_device(): lax.ppermute(object_slices, 'depth', [(d, d + 1) for d in range(depths -...  4.47 us
    ppermute x3, starting transfers between devices, per_device(): brought.append(on_chip(lax.ppermute(packed[k], 'tile', turned(k))))  4.41 us
  transfers between devices with their start and end apart: 10, of which 3 were waited for; matrix products, arithmetic and copies ran while one was open for 0% of the time, Pallas kernels for 28%

profile of v1, /device:TPU:1, one launch (start us, length us, event | category | flops | bytes accessed | tf_op | source)
XLA Modules:
  0.0 65.7 jit_solution(18214080906275152565)
XLA Ops:
  0.0 0.0 collective-permute-start.1
  0.0 4.5 %collective-permute-start = (bf16[2,2,384,384]{3,2,1,0:T(8,128)(2,1)}, bf16[2,2,384,384]{3,2,1,0:T(8,128)(2,1)S(1)}, u32[]{:S(2)}, u32[]{:S(2)}) collective-permute-start(bf16[2,2,384,384]{3,2,1,0:T(8,128)(2,1)} %slab_ref.1), channel_id=1, source_target_pairs={{0,4},{4,8},{8,12},{12,16},{16,20},{20,24},{24,28},{1,5},{5,9},{9,... | collective-permute-start | bytes 3538952 | tf_op jit(solution)/shard_map/ppermute | solution.py:408
  4.5 2.7 %pack.1 = (s16[2,272,128]{2,1,0:T(8,128)(2,1)S(1)}, s16[2,272,128]{2,1,0:T(8,128)(2,1)S(1)}, s16[2,272,128]{2,1,0:T(8,128)(2,1)S(1)}, s16[2,272,128]{2,1,0:T(8,128)(2,1)S(1)}) custom-call(s32[1,3,8,11]{3,2,1,0:T(8,128)} %bitcast.5, s32[1,11]{1,0:T(1,128)} %bitcast.7, f32[8,2,128,128]{3,2,1,0:T(8,128)} %bitcast.4), custom_call_target="tpu_custom_call" | custom-call | tf_op jit(solution)/shard_map/pack/pallas_call | solution.py:409
  7.2 1.1 %collective-permute-start.2 = (s16[2,272,128]{2,1,0:T(8,128)(2,1)S(1)}, s16[2,272,128]{2,1,0:T(8,128)(2,1)S(1)}, u32[]{:S(2)}, u32[]{:S(2)}) collective-permute-start(s16[2,272,128]{2,1,0:T(8,128)(2,1)S(1)} %get-tuple-element.22), channel_id=1, source_target_pairs={{0,1},{1,2},{2,3},{3,0},{4,5},{5,6},{6,7},{7,4},{8,9},{9,10},{10,1... | collective-permute-start | bytes 417800 | tf_op jit(solution)/shard_map/ppermute | solution.py:434
  8.4 2.4 %collective-permute-start.5 = (s16[2,272,128]{2,1,0:T(8,128)(2,1)S(1)}, s16[2,272,128]{2,1,0:T(8,128)(2,1)S(1)}, u32[]{:S(2)}, u32[]{:S(2)}) collective-permute-start(s16[2,272,128]{2,1,0:T(8,128)(2,1)S(1)} %get-tuple-element.25), channel_id=1, source_target_pairs={{0,2},{1,3},{2,0},{3,1},{4,6},{5,7},{6,4},{7,5},{8,10},{9,11},{10,... | collective-permute-start | bytes 417800 | tf_op jit(solution)/shard_map/ppermute | solution.py:434
  10.8 0.9 %collective-permute-start.6 = (s16[2,272,128]{2,1,0:T(8,128)(2,1)S(1)}, s16[2,272,128]{2,1,0:T(8,128)(2,1)S(1)}, u32[]{:S(2)}, u32[]{:S(2)}) collective-permute-start(s16[2,272,128]{2,1,0:T(8,128)(2,1)S(1)} %get-tuple-element.26), channel_id=1, source_target_pairs={{0,3},{1,0},{2,1},{3,2},{4,7},{5,4},{6,5},{7,6},{8,11},{9,8},{10,9... | collective-permute-start | bytes 417800 | tf_op jit(solution)/shard_map/ppermute | solution.py:434
  11.7 1.5 %prep.1 = (bf16[2,2,384,384]{3,2,1,0:T(8,128)(2,1)S(1)}, bf16[768,256]{1,0:T(8,128)(2,1)S(1)}, bf16[256,768]{1,0:T(8,128)(2,1)S(1)}, f32[2,128,128]{2,1,0:T(8,128)S(1)}) custom-call(bf16[2,2,384,384]{3,2,1,0:T(8,128)(2,1)} %slab_ref.1, bf16[768,256]{1,0:T(8,128)(2,1)} %constant.4.clone.right_ref, bf16[256,768]{1,0:T(8,128)(2,1)} %constant.5.clone.left_ref, ...), custom_call_target="tpu_custom_call" | custom-call | tf_op jit(solution)/shard_map/prep/pallas_call | solution.py:419
  13.2 1.6 %collective-permute-done.2.refs_1_ = s16[2,272,128]{2,1,0:T(8,128)(2,1)S(1)} collective-permute-done((s16[2,272,128]{2,1,0:T(8,128)(2,1)S(1)}, s16[2,272,128]{2,1,0:T(8,128)(2,1)S(1)}, u32[]{:S(2)}, u32[]{:S(2)}) %collective-permute-start.2) | collective-permute-done | bytes 139296 | tf_op jit(solution)/shard_map/ppermute | solution.py:434
  14.8 10.9 %collective-permute-done.1.next_ref = bf16[2,2,384,384]{3,2,1,0:T(8,128)(2,1)S(1)} collective-permute-done((bf16[2,2,384,384]{3,2,1,0:T(8,128)(2,1)}, bf16[2,2,384,384]{3,2,1,0:T(8,128)(2,1)S(1)}, u32[]{:S(2)}, u32[]{:S(2)}) %collective-permute-start.1) | collective-permute-done | bytes 1179680 | tf_op jit(solution)/shard_map/ppermute | solution.py:407
  25.7 0.6 shard_map.73
  26.3 8.2 %collective-permute-start.3 = (s16[4,272,128]{2,1,0:T(8,128)(2,1)S(1)}, s16[4,272,128]{2,1,0:T(8,128)(2,1)S(1)}, u32[]{:S(2)}, u32[]{:S(2)}) collective-permute-start(s16[4,272,128]{2,1,0:T(8,128)(2,1)S(1)} %shard_map.73), channel_id=1, source_target_pairs={{0,12},{4,16},{8,20},{12,24},{16,28},{28,8},{1,13},{5,17},{9,21},{... | collective-permute-start | bytes 835592 | tf_op jit(solution)/shard_map/ppermute | solution.py:458
  34.5 0.0 collective-permute-done.5.refs_0_
  34.5 0.0 collective-permute-done.6.refs_1_
  34.5 4.4 %shard_map.75 = s16[4,272,128]{2,1,0:T(8,128)(2,1)S(1)} custom-call(bf16[2,2,384,384]{3,2,1,0:T(8,128)(2,1)S(1)} %get-tuple-element.17.own_ref, bf16[2,2,384,384]{3,2,1,0:T(8,128)(2,1)S(1)} %collective-permute-done.1.next_ref, f32[2,128,128]{2,1,0:T(8,128)S(1)} %get-tuple-element.18.probe_ref, bf16[768,256]{1,0:T(8,128)(2,1)S(1)} %get-tuple-element.19.right_ref, ...), custom_call_target="tpu_custom_call" | custom-call | flops 1610612736 | tf_op jit(solution)/shard_map/pallas_call | solution.py:448
  38.9 1.3 %collective-permute-start.7 = (s16[4,272,128]{2,1,0:T(8,128)(2,1)S(1)}, s16[4,272,128]{2,1,0:T(8,128)(2,1)S(1)}, u32[]{:S(2)}, u32[]{:S(2)}) collective-permute-start(s16[4,272,128]{2,1,0:T(8,128)(2,1)S(1)} %shard_map.75), channel_id=1, source_target_pairs={{0,12},{4,16},{8,20},{12,24},{16,28},{28,8},{1,13},{5,17},{9,21},{... | collective-permute-start | bytes 835592 | tf_op jit(solution)/shard_map/ppermute | solution.py:458
  40.2 0.0 collective-permute-done.last_ref
  40.2 0.0 collective-permute-done.3.arrived_ref
  40.2 4.4 %shard_map.74 = (s16[2,272,128]{2,1,0:T(8,128)(2,1)S(1)}, s16[2,272,128]{2,1,0:T(8,128)(2,1)S(1)}) custom-call(bf16[2,2,384,384]{3,2,1,0:T(8,128)(2,1)S(1)} %collective-permute-done.last_ref, bf16[2,2,384,384]{3,2,1,0:T(8,128)(2,1)S(1)} %get-tuple-element.17.own_ref, f32[2,128,128]{2,1,0:T(8,128)S(1)} %get-tuple-element.18.probe_ref, ...), custom_call_target="tpu_custom_call" | custom-call | flops 1610612736 | tf_op jit(solution)/shard_map/pallas_call | solution.py:461
  44.7 6.0 %collective-permute-start.4 = (s16[2,272,128]{2,1,0:T(8,128)(2,1)S(1)}, s16[2,272,128]{2,1,0:T(8,128)(2,1)S(1)}, u32[]{:S(2)}, u32[]{:S(2)}) collective-permute-start(s16[2,272,128]{2,1,0:T(8,128)(2,1)S(1)} %get-tuple-element.24), channel_id=1, source_target_pairs={{0,3},{1,0},{2,1},{3,2},{4,7},{5,4},{6,5},{7,6},{8,11},{9,8},{10,9... | collective-permute-start | bytes 417800 | tf_op jit(solution)/shard_map/ppermute | solution.py:474
  50.7 0.0 collective-permute-done.7.arrived_ref
  50.7 4.8 %shard_map.76 = (s16[2,272,128]{2,1,0:T(8,128)(2,1)S(1)}, s16[2,272,128]{2,1,0:T(8,128)(2,1)S(1)}) custom-call(bf16[2,2,384,384]{3,2,1,0:T(8,128)(2,1)S(1)} %collective-permute-done.last_ref, bf16[2,2,384,384]{3,2,1,0:T(8,128)(2,1)S(1)} %get-tuple-element.17.own_ref, f32[2,128,128]{2,1,0:T(8,128)S(1)} %get-tuple-element.18.probe_ref, ...), custom_call_target="tpu_custom_call" | custom-call | flops 1610612736 | tf_op jit(solution)/shard_map/pallas_call | solution.py:461
  55.5 0.1 collective-permute-start.8
  55.6 0.1 collective-permute-start.9
  55.7 0.0 collective-permute-done.4.refs_1_
  55.7 7.9 %collective-permute-done.8.refs_2_ = s16[2,272,128]{2,1,0:T(8,128)(2,1)S(1)} collective-permute-done((s16[2,272,128]{2,1,0:T(8,128)(2,1)S(1)}, s16[2,272,128]{2,1,0:T(8,128)(2,1)S(1)}, u32[]{:S(2)}, u32[]{:S(2)}) %collective-permute-start.8) | collective-permute-done | bytes 139296 | tf_op jit(solution)/shard_map/ppermute | solution.py:474
  63.6 0.0 collective-permute-done.9.refs_3_
  63.6 1.9 %unpack.1 = f32[8,2,128,128]{3,2,1,0:T(8,128)} custom-call(s32[1,3,8,11]{3,2,1,0:T(8,128)} %bitcast.6, s32[1,11]{1,0:T(1,128)} %bitcast.8, s16[2,272,128]{2,1,0:T(8,128)(2,1)S(1)} %get-tuple-element.23.refs_0_, s16[2,272,128]{2,1,0:T(8,128)(2,1)S(1)} %collective-permute-done.4.refs_1_, s16[2,272,128]{2,1,0:T(8,128)(2,1)S(1)} %collective-permute-done.8.refs_2_, ...), custom_call_target="tpu_custom_call" | custom-call | tf_op jit(solution)/shard_map/unpack/pallas_call | solution.py:475
Async XLA Ops:
  0.0 25.6 %collective-permute-start.1 = (bf16[2,2,384,384]{3,2,1,0:T(8,128)(2,1)}, bf16[2,2,384,384]{3,2,1,0:T(8,128)(2,1)S(1)}, u32[]{:S(2)}, u32[]{:S(2)}) collective-permute-start(bf16[2,2,384,384]{3,2,1,0:T(8,128)(2,1)} %slab_ref.1), channel_id=1, source_target_pairs={{4,0},{8,4},{12,8},{16,12},{20,16},{24,20},{28,24},{0,28},{5,1},{9... | collective-permute-start | bytes 3538952 | tf_op jit(solution)/shard_map/ppermute | solution.py:407
  0.0 40.2 %collective-permute-start = (bf16[2,2,384,384]{3,2,1,0:T(8,128)(2,1)}, bf16[2,2,384,384]{3,2,1,0:T(8,128)(2,1)S(1)}, u32[]{:S(2)}, u32[]{:S(2)}) collective-permute-start(bf16[2,2,384,384]{3,2,1,0:T(8,128)(2,1)} %slab_ref.1), channel_id=1, source_target_pairs={{0,4},{4,8},{8,12},{12,16},{16,20},{20,24},{24,28},{1,5},{5,9},{9,... | collective-permute-start | bytes 3538952 | tf_op jit(solution)/shard_map/ppermute | solution.py:408
  7.2 7.6 %collective-permute-start.2 = (s16[2,272,128]{2,1,0:T(8,128)(2,1)S(1)}, s16[2,272,128]{2,1,0:T(8,128)(2,1)S(1)}, u32[]{:S(2)}, u32[]{:S(2)}) collective-permute-start(s16[2,272,128]{2,1,0:T(8,128)(2,1)S(1)} %get-tuple-element.22), channel_id=1, source_target_pairs={{0,1},{1,2},{2,3},{3,0},{4,5},{5,6},{6,7},{7,4},{8,9},{9,10},{10,1... | collective-permute-start | bytes 417800 | tf_op jit(solution)/shard_map/ppermute | solution.py:434
  8.4 26.1 %collective-permute-start.5 = (s16[2,272,128]{2,1,0:T(8,128)(2,1)S(1)}, s16[2,272,128]{2,1,0:T(8,128)(2,1)S(1)}, u32[]{:S(2)}, u32[]{:S(2)}) collective-permute-start(s16[2,272,128]{2,1,0:T(8,128)(2,1)S(1)} %get-tuple-element.25), channel_id=1, source_target_pairs={{0,2},{1,3},{2,0},{3,1},{4,6},{5,7},{6,4},{7,5},{8,10},{9,11},{10,... | collective-permute-start | bytes 417800 | tf_op jit(solution)/shard_map/ppermute | solution.py:434
  10.8 23.7 %collective-permute-start.6 = (s16[2,272,128]{2,1,0:T(8,128)(2,1)S(1)}, s16[2,272,128]{2,1,0:T(8,128)(2,1)S(1)}, u32[]{:S(2)}, u32[]{:S(2)}) collective-permute-start(s16[2,272,128]{2,1,0:T(8,128)(2,1)S(1)} %get-tuple-element.26), channel_id=1, source_target_pairs={{0,3},{1,0},{2,1},{3,2},{4,7},{5,4},{6,5},{7,6},{8,11},{9,8},{10,9... | collective-permute-start | bytes 417800 | tf_op jit(solution)/shard_map/ppermute | solution.py:434
  26.3 14.0 %collective-permute-start.3 = (s16[4,272,128]{2,1,0:T(8,128)(2,1)S(1)}, s16[4,272,128]{2,1,0:T(8,128)(2,1)S(1)}, u32[]{:S(2)}, u32[]{:S(2)}) collective-permute-start(s16[4,272,128]{2,1,0:T(8,128)(2,1)S(1)} %shard_map.73), channel_id=1, source_target_pairs={{0,12},{4,16},{8,20},{12,24},{16,28},{28,8},{1,13},{5,17},{9,21},{... | collective-permute-start | bytes 835592 | tf_op jit(solution)/shard_map/ppermute | solution.py:458
  38.9 11.8 %collective-permute-start.7 = (s16[4,272,128]{2,1,0:T(8,128)(2,1)S(1)}, s16[4,272,128]{2,1,0:T(8,128)(2,1)S(1)}, u32[]{:S(2)}, u32[]{:S(2)}) collective-permute-start(s16[4,272,128]{2,1,0:T(8,128)(2,1)S(1)} %shard_map.75), channel_id=1, source_target_pairs={{0,12},{4,16},{8,20},{12,24},{16,28},{28,8},{1,13},{5,17},{9,21},{... | collective-permute-start | bytes 835592 | tf_op jit(solution)/shard_map/ppermute | solution.py:458
  44.7 11.0 %collective-permute-start.4 = (s16[2,272,128]{2,1,0:T(8,128)(2,1)S(1)}, s16[2,272,128]{2,1,0:T(8,128)(2,1)S(1)}, u32[]{:S(2)}, u32[]{:S(2)}) collective-permute-start(s16[2,272,128]{2,1,0:T(8,128)(2,1)S(1)} %get-tuple-element.24), channel_id=1, source_target_pairs={{0,3},{1,0},{2,1},{3,2},{4,7},{5,4},{6,5},{7,6},{8,11},{9,8},{10,9... | collective-permute-start | bytes 417800 | tf_op jit(solution)/shard_map/ppermute | solution.py:474
  55.5 8.1 %collective-permute-start.8 = (s16[2,272,128]{2,1,0:T(8,128)(2,1)S(1)}, s16[2,272,128]{2,1,0:T(8,128)(2,1)S(1)}, u32[]{:S(2)}, u32[]{:S(2)}) collective-permute-start(s16[2,272,128]{2,1,0:T(8,128)(2,1)S(1)} %get-tuple-element.27), channel_id=1, source_target_pairs={{0,2},{1,3},{2,0},{3,1},{4,6},{5,7},{6,4},{7,5},{8,10},{9,11},{10,... | collective-permute-start | bytes 417800 | tf_op jit(solution)/shard_map/ppermute | solution.py:474
  55.6 8.0 %collective-permute-start.9 = (s16[2,272,128]{2,1,0:T(8,128)(2,1)S(1)}, s16[2,272,128]{2,1,0:T(8,128)(2,1)S(1)}, u32[]{:S(2)}, u32[]{:S(2)}) collective-permute-start(s16[2,272,128]{2,1,0:T(8,128)(2,1)S(1)} %get-tuple-element.28), channel_id=1, source_target_pairs={{0,1},{1,2},{2,3},{3,0},{4,5},{5,6},{6,7},{7,4},{8,9},{9,10},{10,1... | collective-permute-start | bytes 417800 | tf_op jit(solution)/shard_map/ppermute | solution.py:474

commit v2 on v1

--- a/solution.py
+++ b/solution.py
@@ -16,6 +16,7 @@
 EXTRA = 16
 PLACES = 4
 SPAN = 16
+ROWS = 16
 GROUP = 4
 
 HBM = pl.BlockSpec(memory_space=pltpu.MemorySpace.HBM)
@@ -42,6 +43,7 @@
     left_high, left_low = halves(right.T)
     right3 = np.concatenate([right_high, right_high, right_low], axis=0)
     left3 = np.concatenate([left_high, left_high, left_low], axis=1)
+    left3 = left3.reshape(2, width // ROWS, ROWS, -1).swapaxes(0, 1).reshape(left3.shape)
     return right3, left3
 
 
@@ -91,7 +93,8 @@
 
 def batches():
     depth, depths = lax.axis_index("depth"), lax.axis_size("depth")
-    return depths + STEPS - 2 - lax.rem(depth + STEPS - 1, depths), depths + STEPS - 2 - depth
+    latest = depths + STEPS - 2
+    return latest - jnp.minimum(depth + STEPS - 1, depths - 1), latest - lax.rem(depth + 1, depths)
 
 
 def prep_kernel(slab_ref, right_ref, left_ref, probe_ref, *refs):
@@ -159,7 +162,7 @@
     exit_ref, out_sems = refs[tiles + 1 :]
     slots, _, width, _ = out_ref.shape
     own = lax.axis_index("tile")
-    batch = batches()[1]
+    batch = lax.axis_size("depth") + STEPS - 2 - lax.axis_index("depth")
     count = count_ref[0, batch]
 
     def send(p):
@@ -200,9 +203,8 @@
         parts = []
         for b in range(2):
             lanes = pl.ds(pl.multiple_of((block + b) * width, width), width)
-            part = pltpu.roll(slab_ref[layer, plane, pl.ds(start, rows), lanes], turn, 1)
-            parts.append(part.astype(jnp.float32))
-        patch_ref[plane] = jnp.where(lane < width - shift, parts[0], parts[1])
+            parts.append(pltpu.roll(slab_ref[layer, plane, pl.ds(start, rows), lanes], turn, 1))
+        patch_ref[plane] = jnp.where(lane < width - shift, parts[0], parts[1]).astype(jnp.float32)
 
 
 def row_offset(row, width, side):
@@ -218,51 +220,66 @@
         for w in (2 * pair, 2 * pair + 1):
             cut(slab_ref, layer, *places[w], patch_ref.at[turn, w])
 
-    def multiply(which, pair):
+    def multiply(which, pair, n, first_row, real, imag):
         turn = which % 2
+        w = 2 * pair + n
+        start = row_offset(places[w][0], width, side) + first_row
+        part = pl.ds(start, real.shape[0])
+        trans_real, trans_imag = patch_ref[turn, w, 0, part, :], patch_ref[turn, w, 1, part, :]
+        rows = slice(n * width + first_row, n * width + first_row + real.shape[0])
+        for plane, value in enumerate((real * trans_real - imag * trans_imag, real * trans_imag + imag * trans_real)):
+            high, low = split(value)
+            x_refs[pair][rows, plane * width : (plane + 1) * width] = high
+            x_refs[pair][rows, (2 + plane) * width : (3 + plane) * width] = low
+
+    def enter(which, pair):
         for n in range(2):
-            w = 2 * pair + n
-            rows = slice(w * width, (w + 1) * width)
-            part = pl.ds(row_offset(places[w][0], width, side), width)
-            real, imag = wave_ref[rows, :width], wave_ref[rows, width:]
-            trans_real, trans_imag = patch_ref[turn, w, 0, part, :], patch_ref[turn, w, 1, part, :]
-            rows = slice(n * width, (n + 1) * width)
-            for plane, value in enumerate((real * trans_real - imag * trans_imag, real * trans_imag + imag * trans_real)):
-                high, low = split(value)
-                x_refs[pair][rows, plane * width : (plane + 1) * width] = high
-                x_refs[pair][rows, (2 + plane) * width : (3 + plane) * width] = low
+            rows = slice((2 * pair + n) * width, (2 * pair + n + 1) * width)
+            multiply(which, pair, n, 0, wave_ref[rows, :width], wave_ref[rows, width:])
 
     def right(pair):
-        x = x_refs[pair][...]
-        x = jnp.concatenate([x, x[:, : 2 * width]], axis=1)
-        spread = jnp.dot(x, right_ref[...], preferred_element_type=jnp.float32)
+        spreads = []
         for n in range(2):
+            x = x_refs[pair][n * width : (n + 1) * width]
+            x = jnp.concatenate([x, x[:, : 2 * width]], axis=1)
+            spreads.append(jnp.dot(x, right_ref[...], preferred_element_type=jnp.float32))
+        for n, spread in enumerate(spreads):
             lanes = slice(n * width, (n + 1) * width)
-            for plane in range(2):
-                high, low = split(spread[n * width : (n + 1) * width, plane * width : (plane + 1) * width])
-                y_refs[pair][plane * width : (plane + 1) * width, lanes] = high
-                y_refs[pair][(2 + plane) * width : (3 + plane) * width, lanes] = low
-
-    def left(pair):
+            for b in range(width // ROWS):
+                for plane in range(2):
+                    rows = slice(b * ROWS, (b + 1) * ROWS)
+                    high, low = split(spread[rows, plane * width : (plane + 1) * width])
+                    start = plane * width + b * ROWS
+                    y_refs[pair][start : start + ROWS, lanes] = high
+                    y_refs[pair][2 * width + start : 2 * width + start + ROWS, lanes] = low
+
+    def left(pair, ahead):
         y = y_refs[pair][...]
         y = jnp.concatenate([y, y[: 2 * width]], axis=0)
-        out = jnp.dot(left_ref[...], y, preferred_element_type=jnp.float32)
-        for n in range(2):
-            w = 2 * pair + n
-            rows = slice(w * width, (w + 1) * width)
-            lanes = slice(n * width, (n + 1) * width)
-            wave_ref[rows, :width] = out[:width, lanes]
-            wave_ref[rows, width:] = out[width:, lanes]
-
-    def one(which):
-        for pair in range(GROUP // 2):
-            multiply(which, pair)
+        outs = [
+            jnp.dot(left_ref[half * width : (half + 1) * width], y, preferred_element_type=jnp.float32)
+            for half in range(2)
+        ]
+        for b in range(width // ROWS):
+            out, c = outs[2 * b // (width // ROWS)], b % (width // ROWS // 2)
+            for n in range(2):
+                lanes = slice(n * width, (n + 1) * width)
+                real = out[2 * c * ROWS : (2 * c + 1) * ROWS, lanes]
+                imag = out[(2 * c + 1) * ROWS : (2 * c + 2) * ROWS, lanes]
+                if ahead is None:
+                    rows = slice((2 * pair + n) * width + b * ROWS, (2 * pair + n) * width + (b + 1) * ROWS)
+                    wave_ref[rows, :width] = real
+                    wave_ref[rows, width:] = imag
+                else:
+                    multiply(ahead, pair, n, b * ROWS, real, imag)
+
+    def one(which, ends):
         for pair in range(GROUP // 2):
             right(pair)
             if which + 1 < len(steps):
                 fill(which + 1, 1 - which % 2, pair)
         for pair in range(GROUP // 2):
-            left(pair)
+            left(pair, None if ends else which + 1)
 
     which = 0
     while which < len(steps):
@@ -275,8 +292,10 @@
             if block[0] == 0:
                 for pair in range(GROUP // 2):
                     fill(0, 0, pair)
+            for pair in range(GROUP // 2):
+                enter(block[0], pair)
             for step in block:
-                one(step)
+                one(step, step == block[-1])
 
         if condition is None:
             run()
@@ -325,19 +344,39 @@
     store(2 * width, extra_rows(codes, jnp.zeros((1, width), jnp.float32)))
 
 
-def first_kernel(ks, pair, own_ref, next_ref, probe_ref, right_ref, left_ref, *refs):
+def first_kernel(ks, pair, own_ref, next_ref, right_ref, left_ref, *refs):
     in_refs, move_ref = refs[: len(ks)], refs[len(ks)]
     column_ref, place_ref, sem, wave_ref, patch_ref, *buffers = refs[len(ks) + 1 :]
     width = right_ref.shape[1] // 2
     depth, depths = lax.axis_index("depth"), lax.axis_size("depth")
-    fresh = depth == depths - 1
     live, places = read_places(in_refs, 0, pair, column_ref, place_ref, sem)
     some = functools.reduce(jnp.logical_or, live)
 
-    @pl.when(some & jnp.logical_or(fresh, depth + STEPS - 1 < depths))
+    @pl.when(some & (depth + STEPS - 1 < depths))
     def _():
         for j in range(GROUP):
             source = in_refs[j // pair]
+            wave_to(wave_ref, j, width, *decode(lambda row, size: source[j % pair, row : row + size, :], width))
+        even = lax.rem(depth, 2) == 0
+        steps = [(own_ref, 0, None), (own_ref, 1, None), (next_ref, 0, even), (next_ref, 1, even)]
+        run_layers(steps, places, wave_ref, patch_ref, buffers[:2], buffers[2:], right_ref, left_ref)
+        for j in range(GROUP):
+            pl.when(live[j])(lambda j=j: send_wave(wave_ref, j, width, move_ref, j))
+
+
+def second_kernel(ks, pair, last_ref, own_ref, next_ref, probe_ref, right_ref, left_ref, arrived_ref, *refs):
+    in_refs, out_refs = refs[: len(ks)], refs[len(ks) : 2 * len(ks)]
+    column_ref, place_ref, sem, wave_ref, patch_ref, *buffers = refs[2 * len(ks) :]
+    width = right_ref.shape[1] // 2
+    depth, depths = lax.axis_index("depth"), lax.axis_size("depth")
+    live, places = read_places(in_refs, 1, pair, column_ref, place_ref, sem)
+    some = functools.reduce(jnp.logical_or, live)
+
+    @pl.when(some)
+    def _():
+        final = depth == depths - 1
+        fresh = jnp.logical_or(depth < 2, final)
+        for j in range(GROUP):
 
             @pl.when(fresh)
             def _():
@@ -345,38 +384,12 @@
 
             @pl.when(jnp.logical_not(fresh))
             def _():
-                wave_to(wave_ref, j, width, *decode(lambda row, size: source[j % pair, row : row + size, :], width))
-
-        own = jnp.logical_not(fresh)
-        steps = [(own_ref, 0, own), (own_ref, 1, own), (next_ref, 0, None), (next_ref, 1, None)]
-        run_layers(steps, places, wave_ref, patch_ref, buffers[:2], buffers[2:], right_ref, left_ref)
-        for j in range(GROUP):
-            pl.when(live[j])(lambda j=j: send_wave(wave_ref, j, width, move_ref, j))
-
-
-def second_kernel(ks, pair, last_ref, own_ref, probe_ref, right_ref, left_ref, arrived_ref, *refs):
-    in_refs, out_refs = refs[: len(ks)], refs[len(ks) : 2 * len(ks)]
-    column_ref, place_ref, sem, wave_ref, patch_ref, *buffers = refs[2 * len(ks) :]
-    width = right_ref.shape[1] // 2
-    depth = lax.axis_index("depth")
-    live, places = read_places(in_refs, 1, pair, column_ref, place_ref, sem)
-    some = functools.reduce(jnp.logical_or, live)
-
-    @pl.when(some)
-    def _():
-        fresh = depth < STEPS - 2
-        for j in range(GROUP):
-
-            @pl.when(fresh)
-            def _():
-                wave_to(wave_ref, j, width, probe_ref[0], probe_ref[1])
-
-            @pl.when(jnp.logical_not(fresh))
-            def _():
                 wave_to(wave_ref, j, width, *decode(lambda row, size: arrived_ref[j, row : row + size, :], width))
 
-        near = depth >= 1
-        steps = [(last_ref, 0, near), (last_ref, 1, near), (own_ref, 0, None), (own_ref, 1, None)]
+        inner = jnp.logical_not(final)
+        below = inner & (lax.rem(depth, 2) == 1)
+        steps = [(last_ref, 0, below), (last_ref, 1, below), (own_ref, 0, inner), (own_ref, 1, inner)]
+        steps += [(next_ref, 0, None), (next_ref, 1, None)]
         run_layers(steps, places, wave_ref, patch_ref, buffers[:2], buffers[2:], right_ref, left_ref)
         for j in range(GROUP):
             pl.when(live[j])(lambda j=j: send_wave(wave_ref, j, width, out_refs[j // pair], j % pair))
@@ -405,7 +418,7 @@
     lists = [off_chip(value) for value in lists]
 
     next_slab = on_chip(lax.ppermute(object_slices, "depth", [((d + 1) % depths, d) for d in range(depths)]))
-    last_slab = on_chip(lax.ppermute(object_slices, "depth", [(d, d + 1) for d in range(depths - 1)]))
+    last_slab = on_chip(lax.ppermute(object_slices, "depth", [(d, d + 1) for d in range(0, depths, 2)]))
     packed = pl.pallas_call(
         functools.partial(pack_kernel, tiles, pair),
         out_shape=[coded] * tiles,
@@ -426,6 +439,9 @@
         name="prep",
     )(*[off_chip(value) for value in kept])
 
+    def flat(depth, tile):
+        return (depth % depths) * tiles + tile % tiles
+
     def turned(k):
         return [(t, (t + k) % tiles) for t in range(tiles)]
 
@@ -448,30 +464,28 @@
         moved = pl.pallas_call(
             functools.partial(first_kernel, ks, pair),
             out_shape=moved_shape,
-            in_specs=[VMEM] * (5 + per_group),
+            in_specs=[VMEM] * (4 + per_group),
             out_specs=VMEM,
             scratch_shapes=scratch,
             cost_estimate=pl.CostEstimate(flops=4 * flops, bytes_accessed=0, transcendentals=0),
             compiler_params=PARAMS,
-        )(own_slab, next_slab, probe, right, left, *[brought[k] for k in ks])
-        pairs = [(d, d + STEPS - 1) for d in range(depths - STEPS + 1)] + [(depths - 1, STEPS - 2)]
+        )(own_slab, next_slab, right, left, *[brought[k] for k in ks])
+        pairs = [(d, d + 2) for d in range(depths - STEPS + 1)]
         arrived.append(on_chip(lax.ppermute(moved, "depth", pairs)))
     back = [None] * tiles
     for g, ks in enumerate(groups):
         outs = pl.pallas_call(
             functools.partial(second_kernel, ks, pair),
             out_shape=[coded] * per_group,
-            in_specs=[VMEM] * (6 + per_group),
+            in_specs=[VMEM] * (7 + per_group),
             out_specs=[VMEM] * per_group,
             scratch_shapes=scratch,
             cost_estimate=pl.CostEstimate(flops=4 * flops, bytes_accessed=0, transcendentals=0),
             compiler_params=PARAMS,
-        )(last_slab, own_slab, probe, right, left, arrived[g], *[brought[k] for k in ks])
+        )(last_slab, own_slab, next_slab, probe, right, left, arrived[g], *[brought[k] for k in ks])
         for k, value in zip(ks, outs):
-            if k == 0:
-                back[k] = value
-            else:
-                back[k] = on_chip(lax.ppermute(value, "tile", turned(-k)))
+            pairs = [(flat(d, t), flat(d + 1, t - k)) for d in range(depths) for t in range(tiles)]
+            back[k] = on_chip(lax.ppermute(value, ("depth", "tile"), pairs))
     exits = pl.pallas_call(
         functools.partial(unpack_kernel, tiles, pair),
         out_shape=jax.ShapeDtypeStruct(fronts.shape[2:], jnp.float32),

time: 66.4 us -> 55.9 us (0.84)
  the two profiles are of different devices: /device:TPU:1 before, /device:TPU:0 now
where the time goes in v2:
time: 55.9 us; the launch traced here: 55.5 us
  starting transfers between devices  29.1 us (52%)
  Pallas kernels  14.6 us (26%)
  waiting for transfers between devices  11.6 us (21%)
    ppermute x2, starting transfers between devices, per_device(): arrived.append(on_chip(lax.ppermute(moved, 'depth', pairs)))  11.5 us
    pallas_call x2, Pallas kernels, per_device(): pl.pallas_call(functools.partial(second_kernel, ks, pair), out_shape=[cod...  7.84 us
    ppermute x4, starting transfers between devices, per_device(): back[k] = on_chip(lax.ppermute(value, ('depth', 'tile'), pairs))  7.76 us
    ppermute x3, waiting for transfers between devices, per_device(): brought.append(on_chip(lax.ppermute(packed[k], 'tile', turned(k))))  6.11 us
    ppermute x3, starting transfers between devices, per_device(): brought.append(on_chip(lax.ppermute(packed[k], 'tile', turned(k))))  5.04 us
    ppermute x4, waiting for transfers between devices, per_device(): back[k] = on_chip(lax.ppermute(value, ('depth', 'tile'), pairs))  4.78 us
    ppermute x1, starting transfers between devices, per_device(): lax.ppermute(object_slices, 'depth', [((d + 1) % depths, d) for d in rang...  3.36 us
    pallas_call x1, Pallas kernels, per_device(): pl.pallas_call(functools.partial(pack_kernel, tiles, pair), out_shape=[co...  2.05 us
  transfers between devices with their start and end apart: 11, of which 4 were waited for; matrix products, arithmetic and copies ran while one was open for 0% of the time, Pallas kernels for 23%

profile of v2, /device:TPU:0, one launch (start us, length us, event | category | flops | bytes accessed | tf_op | source)
XLA Modules:
  0.0 55.5 jit_solution(17586327730860681095)
XLA Ops:
  0.0 3.4 %collective-permute-start.1 = (bf16[2,2,384,384]{3,2,1,0:T(8,128)(2,1)}, bf16[2,2,384,384]{3,2,1,0:T(8,128)(2,1)S(1)}, u32[]{:S(2)}, u32[]{:S(2)}) collective-permute-start(bf16[2,2,384,384]{3,2,1,0:T(8,128)(2,1)} %slab_ref.1), channel_id=1, source_target_pairs={{4,0},{8,4},{12,8},{16,12},{20,16},{24,20},{28,24},{0,28},{5,1},{9... | collective-permute-start | bytes 3538952 | tf_op jit(solution)/shard_map/ppermute | solution.py:420
  3.4 1.4 %collective-permute-start = (bf16[2,2,384,384]{3,2,1,0:T(8,128)(2,1)}, bf16[2,2,384,384]{3,2,1,0:T(8,128)(2,1)S(1)}, u32[]{:S(2)}, u32[]{:S(2)}) collective-permute-start(bf16[2,2,384,384]{3,2,1,0:T(8,128)(2,1)} %slab_ref.1), channel_id=1, source_target_pairs={{0,4},{8,12},{16,20},{24,28},{1,5},{9,13},{17,21},{25,29},{2,6},{1... | collective-permute-start | bytes 3538952 | tf_op jit(solution)/shard_map/ppermute | solution.py:421
  4.7 2.1 %pack.1 = (s16[2,272,128]{2,1,0:T(8,128)(2,1)S(1)}, s16[2,272,128]{2,1,0:T(8,128)(2,1)S(1)}, s16[2,272,128]{2,1,0:T(8,128)(2,1)S(1)}, s16[2,272,128]{2,1,0:T(8,128)(2,1)S(1)}) custom-call(s32[1,3,8,11]{3,2,1,0:T(8,128)} %bitcast.5, s32[1,11]{1,0:T(1,128)} %bitcast.7, f32[8,2,128,128]{3,2,1,0:T(8,128)} %bitcast.4), custom_call_target="tpu_custom_call" | custom-call | tf_op jit(solution)/shard_map/pack/pallas_call | solution.py:422
  6.8 3.0 %collective-permute-start.6 = (s16[2,272,128]{2,1,0:T(8,128)(2,1)S(1)}, s16[2,272,128]{2,1,0:T(8,128)(2,1)S(1)}, u32[]{:S(2)}, u32[]{:S(2)}) collective-permute-start(s16[2,272,128]{2,1,0:T(8,128)(2,1)S(1)} %get-tuple-element.25), channel_id=1, source_target_pairs={{0,2},{1,3},{2,0},{3,1},{4,6},{5,7},{6,4},{7,5},{8,10},{9,11},{10,... | collective-permute-start | bytes 417800 | tf_op jit(solution)/shard_map/ppermute | solution.py:450
  9.8 1.0 %collective-permute-start.7 = (s16[2,272,128]{2,1,0:T(8,128)(2,1)S(1)}, s16[2,272,128]{2,1,0:T(8,128)(2,1)S(1)}, u32[]{:S(2)}, u32[]{:S(2)}) collective-permute-start(s16[2,272,128]{2,1,0:T(8,128)(2,1)S(1)} %get-tuple-element.26), channel_id=1, source_target_pairs={{0,3},{1,0},{2,1},{3,2},{4,7},{5,4},{6,5},{7,6},{8,11},{9,8},{10,9... | collective-permute-start | bytes 417800 | tf_op jit(solution)/shard_map/ppermute | solution.py:450
  10.8 1.0 %collective-permute-start.2 = (s16[2,272,128]{2,1,0:T(8,128)(2,1)S(1)}, s16[2,272,128]{2,1,0:T(8,128)(2,1)S(1)}, u32[]{:S(2)}, u32[]{:S(2)}) collective-permute-start(s16[2,272,128]{2,1,0:T(8,128)(2,1)S(1)} %get-tuple-element.22), channel_id=1, source_target_pairs={{0,1},{1,2},{2,3},{3,0},{4,5},{5,6},{6,7},{7,4},{8,9},{9,10},{10,1... | collective-permute-start | bytes 417800 | tf_op jit(solution)/shard_map/ppermute | solution.py:450
  11.8 1.5 %prep.1 = (bf16[2,2,384,384]{3,2,1,0:T(8,128)(2,1)S(1)}, bf16[768,256]{1,0:T(8,128)(2,1)S(1)}, bf16[256,768]{1,0:T(8,128)(2,1)S(1)}, f32[2,128,128]{2,1,0:T(8,128)S(1)}) custom-call(bf16[2,2,384,384]{3,2,1,0:T(8,128)(2,1)} %slab_ref.1, bf16[768,256]{1,0:T(8,128)(2,1)} %constant.4.clone.right_ref, bf16[256,768]{1,0:T(8,128)(2,1)} %constant.5.clone.left_ref, ...), custom_call_target="tpu_custom_call" | custom-call | tf_op jit(solution)/shard_map/prep/pallas_call | solution.py:432
  13.4 6.1 %collective-permute-done.6.refs_0_ = s16[2,272,128]{2,1,0:T(8,128)(2,1)S(1)} collective-permute-done((s16[2,272,128]{2,1,0:T(8,128)(2,1)S(1)}, s16[2,272,128]{2,1,0:T(8,128)(2,1)S(1)}, u32[]{:S(2)}, u32[]{:S(2)}) %collective-permute-start.6) | collective-permute-done | bytes 139296 | tf_op jit(solution)/shard_map/ppermute | solution.py:450
  19.5 0.0 collective-permute-done.7.refs_1_
  19.5 0.0 collective-permute-done.1.next_ref
  19.5 0.6 %shard_map.75 = s16[4,272,128]{2,1,0:T(8,128)(2,1)S(1)} custom-call(bf16[2,2,384,384]{3,2,1,0:T(8,128)(2,1)S(1)} %get-tuple-element.17.own_ref, bf16[2,2,384,384]{3,2,1,0:T(8,128)(2,1)S(1)} %collective-permute-done.1.next_ref, bf16[768,256]{1,0:T(8,128)(2,1)S(1)} %get-tuple-element.19.right_ref, bf16[256,768]{1,0:T(8,128)(2,1)S(1)} %get-tuple-element.20.left_ref, ...), custom_call_target="tpu_custom_call" | custom-call | flops 1610612736 | tf_op jit(solution)/shard_map/pallas_call | solution.py:464
  20.1 6.6 %collective-permute-start.8 = (s16[4,272,128]{2,1,0:T(8,128)(2,1)S(1)}, s16[4,272,128]{2,1,0:T(8,128)(2,1)S(1)}, u32[]{:S(2)}, u32[]{:S(2)}) collective-permute-start(s16[4,272,128]{2,1,0:T(8,128)(2,1)S(1)} %shard_map.75), channel_id=1, source_target_pairs={{0,8},{4,12},{8,16},{12,20},{16,24},{1,9},{5,13},{9,17},{13,21},{1... | collective-permute-start | bytes 835592 | tf_op jit(solution)/shard_map/ppermute | solution.py:474
  26.7 0.0 collective-permute-done.2.refs_1_
  26.7 0.6 %shard_map.73 = s16[4,272,128]{2,1,0:T(8,128)(2,1)S(1)} custom-call(bf16[2,2,384,384]{3,2,1,0:T(8,128)(2,1)S(1)} %get-tuple-element.17.own_ref, bf16[2,2,384,384]{3,2,1,0:T(8,128)(2,1)S(1)} %collective-permute-done.1.next_ref, bf16[768,256]{1,0:T(8,128)(2,1)S(1)} %get-tuple-element.19.right_ref, bf16[256,768]{1,0:T(8,128)(2,1)S(1)} %get-tuple-element.20.left_ref, ...), custom_call_target="tpu_custom_call" | custom-call | flops 1610612736 | tf_op jit(solution)/shard_map/pallas_call | solution.py:464
  27.3 5.0 %collective-permute-start.3 = (s16[4,272,128]{2,1,0:T(8,128)(2,1)S(1)}, s16[4,272,128]{2,1,0:T(8,128)(2,1)S(1)}, u32[]{:S(2)}, u32[]{:S(2)}) collective-permute-start(s16[4,272,128]{2,1,0:T(8,128)(2,1)S(1)} %shard_map.73), channel_id=1, source_target_pairs={{0,8},{4,12},{8,16},{12,20},{16,24},{1,9},{5,13},{9,17},{13,21},{1... | collective-permute-start | bytes 835592 | tf_op jit(solution)/shard_map/ppermute | solution.py:474
  32.3 0.0 collective-permute-done.last_ref
  32.3 0.7 %collective-permute-done.8.arrived_ref = s16[4,272,128]{2,1,0:T(8,128)(2,1)S(1)} collective-permute-done((s16[4,272,128]{2,1,0:T(8,128)(2,1)S(1)}, s16[4,272,128]{2,1,0:T(8,128)(2,1)S(1)}, u32[]{:S(2)}, u32[]{:S(2)}) %collective-permute-start.8) | collective-permute-done | bytes 278560 | tf_op jit(solution)/shard_map/ppermute | solution.py:474
  33.0 3.7 %shard_map.76 = (s16[2,272,128]{2,1,0:T(8,128)(2,1)S(1)}, s16[2,272,128]{2,1,0:T(8,128)(2,1)S(1)}) custom-call(bf16[2,2,384,384]{3,2,1,0:T(8,128)(2,1)S(1)} %collective-permute-done.last_ref, bf16[2,2,384,384]{3,2,1,0:T(8,128)(2,1)S(1)} %get-tuple-element.17.own_ref, bf16[2,2,384,384]{3,2,1,0:T(8,128)(2,1)S(1)} %collective-permute-done.1.next_ref, ...), custom_call_target="tpu_custom_call" | custom-call | flops 1610612736 | tf_op jit(solution)/shard_map/pallas_call | solution.py:477
  36.8 0.5 collective-permute-start.10
  37.3 1.0 %collective-permute-start.9 = (s16[2,272,128]{2,1,0:T(8,128)(2,1)S(1)}, s16[2,272,128]{2,1,0:T(8,128)(2,1)S(1)}, u32[]{:S(2)}, u32[]{:S(2)}) collective-permute-start(s16[2,272,128]{2,1,0:T(8,128)(2,1)S(1)} %get-tuple-element.27), channel_id=1, source_target_pairs={{0,6},{1,7},{2,4},{3,5},{4,10},{5,11},{6,8},{7,9},{8,14},{9,15},{1... | collective-permute-start | bytes 417800 | tf_op jit(solution)/shard_map/ppermute | solution.py:488
  38.3 0.0 collective-permute-done.3.arrived_ref
  38.3 4.1 %shard_map.74 = (s16[2,272,128]{2,1,0:T(8,128)(2,1)S(1)}, s16[2,272,128]{2,1,0:T(8,128)(2,1)S(1)}) custom-call(bf16[2,2,384,384]{3,2,1,0:T(8,128)(2,1)S(1)} %collective-permute-done.last_ref, bf16[2,2,384,384]{3,2,1,0:T(8,128)(2,1)S(1)} %get-tuple-element.17.own_ref, bf16[2,2,384,384]{3,2,1,0:T(8,128)(2,1)S(1)} %collective-permute-done.1.next_ref, ...), custom_call_target="tpu_custom_call" | custom-call | flops 1610612736 | tf_op jit(solution)/shard_map/pallas_call | solution.py:477
  42.4 3.1 %collective-permute-start.4 = (s16[2,272,128]{2,1,0:T(8,128)(2,1)S(1)}, s16[2,272,128]{2,1,0:T(8,128)(2,1)S(1)}, u32[]{:S(2)}, u32[]{:S(2)}) collective-permute-start(s16[2,272,128]{2,1,0:T(8,128)(2,1)S(1)} %get-tuple-element.23), channel_id=1, source_target_pairs={{0,4},{1,5},{2,6},{3,7},{4,8},{5,9},{6,10},{7,11},{8,12},{9,13},{1... | collective-permute-start | bytes 417800 | tf_op jit(solution)/shard_map/ppermute | solution.py:488
  45.5 3.1 %collective-permute-start.5 = (s16[2,272,128]{2,1,0:T(8,128)(2,1)S(1)}, s16[2,272,128]{2,1,0:T(8,128)(2,1)S(1)}, u32[]{:S(2)}, u32[]{:S(2)}) collective-permute-start(s16[2,272,128]{2,1,0:T(8,128)(2,1)S(1)} %get-tuple-element.24), channel_id=1, source_target_pairs={{0,7},{1,4},{2,5},{3,6},{4,11},{5,8},{6,9},{7,10},{8,15},{9,12},{1... | collective-permute-start | bytes 417800 | tf_op jit(solution)/shard_map/ppermute | solution.py:488
  48.6 0.0 collective-permute-done.10.refs_3_
  48.6 1.4 %collective-permute-done.9.refs_2_ = s16[2,272,128]{2,1,0:T(8,128)(2,1)S(1)} collective-permute-done((s16[2,272,128]{2,1,0:T(8,128)(2,1)S(1)}, s16[2,272,128]{2,1,0:T(8,128)(2,1)S(1)}, u32[]{:S(2)}, u32[]{:S(2)}) %collective-permute-start.9) | collective-permute-done | bytes 139296 | tf_op jit(solution)/shard_map/ppermute | solution.py:488
  50.0 0.0 collective-permute-done.4.refs_0_
  50.0 3.4 %collective-permute-done.5.refs_1_ = s16[2,272,128]{2,1,0:T(8,128)(2,1)S(1)} collective-permute-done((s16[2,272,128]{2,1,0:T(8,128)(2,1)S(1)}, s16[2,272,128]{2,1,0:T(8,128)(2,1)S(1)}, u32[]{:S(2)}, u32[]{:S(2)}) %collective-permute-start.5) | collective-permute-done | bytes 139296 | tf_op jit(solution)/shard_map/ppermute | solution.py:488
  53.4 1.9 %unpack.1 = f32[8,2,128,128]{3,2,1,0:T(8,128)} custom-call(s32[1,3,8,11]{3,2,1,0:T(8,128)} %bitcast.6, s32[1,11]{1,0:T(1,128)} %bitcast.8, s16[2,272,128]{2,1,0:T(8,128)(2,1)S(1)} %collective-permute-done.4.refs_0_, s16[2,272,128]{2,1,0:T(8,128)(2,1)S(1)} %collective-permute-done.5.refs_1_, s16[2,272,128]{2,1,0:T(8,128)(2,1)S(1)} %collective-permute-done.9.refs_2_, ...), custom_call_target="tpu_custom_call" | custom-call | tf_op jit(solution)/shard_map/unpack/pallas_call | solution.py:489
Async XLA Ops:
  0.0 19.5 %collective-permute-start.1 = (bf16[2,2,384,384]{3,2,1,0:T(8,128)(2,1)}, bf16[2,2,384,384]{3,2,1,0:T(8,128)(2,1)S(1)}, u32[]{:S(2)}, u32[]{:S(2)}) collective-permute-start(bf16[2,2,384,384]{3,2,1,0:T(8,128)(2,1)} %slab_ref.1), channel_id=1, source_target_pairs={{4,0},{8,4},{12,8},{16,12},{20,16},{24,20},{28,24},{0,28},{5,1},{9... | collective-permute-start | bytes 3538952 | tf_op jit(solution)/shard_map/ppermute | solution.py:420
  3.4 29.0 %collective-permute-start = (bf16[2,2,384,384]{3,2,1,0:T(8,128)(2,1)}, bf16[2,2,384,384]{3,2,1,0:T(8,128)(2,1)S(1)}, u32[]{:S(2)}, u32[]{:S(2)}) collective-permute-start(bf16[2,2,384,384]{3,2,1,0:T(8,128)(2,1)} %slab_ref.1), channel_id=1, source_target_pairs={{0,4},{8,12},{16,20},{24,28},{1,5},{9,13},{17,21},{25,29},{2,6},{1... | collective-permute-start | bytes 3538952 | tf_op jit(solution)/shard_map/ppermute | solution.py:421
  6.8 12.7 %collective-permute-start.6 = (s16[2,272,128]{2,1,0:T(8,128)(2,1)S(1)}, s16[2,272,128]{2,1,0:T(8,128)(2,1)S(1)}, u32[]{:S(2)}, u32[]{:S(2)}) collective-permute-start(s16[2,272,128]{2,1,0:T(8,128)(2,1)S(1)} %get-tuple-element.25), channel_id=1, source_target_pairs={{0,2},{1,3},{2,0},{3,1},{4,6},{5,7},{6,4},{7,5},{8,10},{9,11},{10,... | collective-permute-start | bytes 417800 | tf_op jit(solution)/shard_map/ppermute | solution.py:450
  9.8 9.7 %collective-permute-start.7 = (s16[2,272,128]{2,1,0:T(8,128)(2,1)S(1)}, s16[2,272,128]{2,1,0:T(8,128)(2,1)S(1)}, u32[]{:S(2)}, u32[]{:S(2)}) collective-permute-start(s16[2,272,128]{2,1,0:T(8,128)(2,1)S(1)} %get-tuple-element.26), channel_id=1, source_target_pairs={{0,3},{1,0},{2,1},{3,2},{4,7},{5,4},{6,5},{7,6},{8,11},{9,8},{10,9... | collective-permute-start | bytes 417800 | tf_op jit(solution)/shard_map/ppermute | solution.py:450
  10.8 15.9 %collective-permute-start.2 = (s16[2,272,128]{2,1,0:T(8,128)(2,1)S(1)}, s16[2,272,128]{2,1,0:T(8,128)(2,1)S(1)}, u32[]{:S(2)}, u32[]{:S(2)}) collective-permute-start(s16[2,272,128]{2,1,0:T(8,128)(2,1)S(1)} %get-tuple-element.22), channel_id=1, source_target_pairs={{0,1},{1,2},{2,3},{3,0},{4,5},{5,6},{6,7},{7,4},{8,9},{9,10},{10,1... | collective-permute-start | bytes 417800 | tf_op jit(solution)/shard_map/ppermute | solution.py:450
  20.1 12.9 %collective-permute-start.8 = (s16[4,272,128]{2,1,0:T(8,128)(2,1)S(1)}, s16[4,272,128]{2,1,0:T(8,128)(2,1)S(1)}, u32[]{:S(2)}, u32[]{:S(2)}) collective-permute-start(s16[4,272,128]{2,1,0:T(8,128)(2,1)S(1)} %shard_map.75), channel_id=1, source_target_pairs={{0,8},{4,12},{8,16},{12,20},{16,24},{1,9},{5,13},{9,17},{13,21},{1... | collective-permute-start | bytes 835592 | tf_op jit(solution)/shard_map/ppermute | solution.py:474
  27.3 11.0 %collective-permute-start.3 = (s16[4,272,128]{2,1,0:T(8,128)(2,1)S(1)}, s16[4,272,128]{2,1,0:T(8,128)(2,1)S(1)}, u32[]{:S(2)}, u32[]{:S(2)}) collective-permute-start(s16[4,272,128]{2,1,0:T(8,128)(2,1)S(1)} %shard_map.73), channel_id=1, source_target_pairs={{0,8},{4,12},{8,16},{12,20},{16,24},{1,9},{5,13},{9,17},{13,21},{1... | collective-permute-start | bytes 835592 | tf_op jit(solution)/shard_map/ppermute | solution.py:474
  36.8 11.9 %collective-permute-start.10 = (s16[2,272,128]{2,1,0:T(8,128)(2,1)S(1)}, s16[2,272,128]{2,1,0:T(8,128)(2,1)S(1)}, u32[]{:S(2)}, u32[]{:S(2)}) collective-permute-start(s16[2,272,128]{2,1,0:T(8,128)(2,1)S(1)} %get-tuple-element.28), channel_id=1, source_target_pairs={{0,5},{1,6},{2,7},{3,4},{4,9},{5,10},{6,11},{7,8},{8,13},{9,14},{1... | collective-permute-start | bytes 417800 | tf_op jit(solution)/shard_map/ppermute | solution.py:488
  37.3 12.7 %collective-permute-start.9 = (s16[2,272,128]{2,1,0:T(8,128)(2,1)S(1)}, s16[2,272,128]{2,1,0:T(8,128)(2,1)S(1)}, u32[]{:S(2)}, u32[]{:S(2)}) collective-permute-start(s16[2,272,128]{2,1,0:T(8,128)(2,1)S(1)} %get-tuple-element.27), channel_id=1, source_target_pairs={{0,6},{1,7},{2,4},{3,5},{4,10},{5,11},{6,8},{7,9},{8,14},{9,15},{1... | collective-permute-start | bytes 417800 | tf_op jit(solution)/shard_map/ppermute | solution.py:488
  42.4 7.6 %collective-permute-start.4 = (s16[2,272,128]{2,1,0:T(8,128)(2,1)S(1)}, s16[2,272,128]{2,1,0:T(8,128)(2,1)S(1)}, u32[]{:S(2)}, u32[]{:S(2)}) collective-permute-start(s16[2,272,128]{2,1,0:T(8,128)(2,1)S(1)} %get-tuple-element.23), channel_id=1, source_target_pairs={{0,4},{1,5},{2,6},{3,7},{4,8},{5,9},{6,10},{7,11},{8,12},{9,13},{1... | collective-permute-start | bytes 417800 | tf_op jit(solution)/shard_map/ppermute | solution.py:488
  45.5 7.9 %collective-permute-start.5 = (s16[2,272,128]{2,1,0:T(8,128)(2,1)S(1)}, s16[2,272,128]{2,1,0:T(8,128)(2,1)S(1)}, u32[]{:S(2)}, u32[]{:S(2)}) collective-permute-start(s16[2,272,128]{2,1,0:T(8,128)(2,1)S(1)} %get-tuple-element.24), channel_id=1, source_target_pairs={{0,7},{1,4},{2,5},{3,6},{4,11},{5,8},{6,9},{7,10},{8,15},{9,12},{1... | collective-permute-start | bytes 417800 | tf_op jit(solution)/shard_map/ppermute | solution.py:488

commit v3 on v2

--- a/solution.py
+++ b/solution.py
@@ -157,9 +157,8 @@
                 store(2 * width, extra_rows((none, none), places))
 
 
-def unpack_kernel(tiles, pair, list_ref, count_ref, *refs):
-    in_refs, out_ref = refs[:tiles], refs[tiles]
-    exit_ref, out_sems = refs[tiles + 1 :]
+def unpack_kernel(tiles, pair, ks, first, list_ref, count_ref, *refs):
+    in_refs, (out_ref, exit_ref, out_sems) = refs[: len(ks)], refs[-3:]
     slots, _, width, _ = out_ref.shape
     own = lax.axis_index("tile")
     batch = lax.axis_size("depth") + STEPS - 2 - lax.axis_index("depth")
@@ -168,27 +167,33 @@
     def send(p):
         return pltpu.make_async_copy(exit_ref.at[p], out_ref.at[p], out_sems.at[p])
 
-    for p in range(slots):
-
-        @pl.when(p >= count)
-        def _():
-            exit_ref[p] = jnp.zeros(exit_ref.shape[1:], jnp.float32)
-            send(p).start()
-
-    for k in range(tiles):
+    if first:
+        for p in range(slots):
+
+            @pl.when(p >= count)
+            def _():
+                exit_ref[p] = jnp.zeros(exit_ref.shape[1:], jnp.float32)
+                send(p).start()
+
+    found = []
+    for n, k in enumerate(ks):
         tile = lax.rem(own + k, tiles)
         for i in range(pair):
             p = nth_of_tile(lambda p: list_ref[0, 0, p, batch], count, slots, tile, i)
+            found.append(p)
 
             @pl.when(p >= 0)
             def _():
-                real, imag = decode(lambda row, size: in_refs[k][i, row : row + size, :], width)
+                real, imag = decode(lambda row, size: in_refs[n][i, row : row + size, :], width)
                 exit_ref[p, 0] = real
                 exit_ref[p, 1] = imag
                 send(p).start()
 
-    for p in range(slots):
-        send(p).wait()
+    for p in found:
+        pl.when(p >= 0)(lambda p=p: send(p).wait())
+    if first:
+        for p in range(slots):
+            pl.when(p >= count)(lambda p=p: send(p).wait())
 
 
 def cut(slab_ref, layer, row, column, patch_ref):
@@ -486,15 +491,18 @@
         for k, value in zip(ks, outs):
             pairs = [(flat(d, t), flat(d + 1, t - k)) for d in range(depths) for t in range(tiles)]
             back[k] = on_chip(lax.ppermute(value, ("depth", "tile"), pairs))
-    exits = pl.pallas_call(
-        functools.partial(unpack_kernel, tiles, pair),
-        out_shape=jax.ShapeDtypeStruct(fronts.shape[2:], jnp.float32),
-        in_specs=[SMEM, SMEM] + [VMEM] * tiles,
-        out_specs=HBM,
-        scratch_shapes=[pltpu.VMEM(fronts.shape[2:], jnp.float32), pltpu.SemaphoreType.DMA((slots,))],
-        compiler_params=PARAMS,
-        name="unpack",
-    )(*lists, *back)
+    exits = None
+    for g, ks in enumerate(groups):
+        before = [] if exits is None else [exits]
+        exits = pl.pallas_call(
+            functools.partial(unpack_kernel, tiles, pair, ks, g == 0),
+            out_shape=jax.ShapeDtypeStruct(fronts.shape[2:], jnp.float32),
+            in_specs=[SMEM, SMEM] + [VMEM] * per_group + [HBM] * len(before),
+            out_specs=HBM,
+            input_output_aliases={2 + per_group: 0} if before else {},
+            scratch_shapes=[pltpu.VMEM(fronts.shape[2:], jnp.float32), pltpu.SemaphoreType.DMA((slots,))],
+            compiler_params=PARAMS,
+        )(*lists, *[back[k] for k in ks], *before)
     return exits[None, None]
 
 

time: 55.9 us -> 55.1 us (0.986)
  waiting for transfers between devices: 11.6 us -> 8.18 us
  Pallas kernels: 14.6 us -> 16.3 us
  starting transfers between devices: 29.1 us -> 30 us
    ppermute x4, waiting for transfers between devices: 4.78 us -> 1.37 us  [per_device(): back[k] = on_chip(lax.ppermute(value, ('depth', 'tile'), pairs))]
    pallas_call x1 -> x2, Pallas kernels: 1.93 us -> 3.6 us  [per_device(): pl.pallas_call(functools.partial(unpack_kernel, tiles, pair, ks, g == 0),...]
    ppermute x4, starting transfers between devices: 7.76 us -> 8.65 us  [per_device(): back[k] = on_chip(lax.ppermute(value, ('depth', 'tile'), pairs))]
  transfers between devices with their start and end apart: 11 -> 11, of which waited for: 4 -> 4; matrix products, arithmetic and copies ran while one was open for 0% -> 0% of each run, Pallas kernels for 23% -> 27%
where the time goes in v3:
time: 55.1 us; the launch traced here: 54.7 us
  starting transfers between devices  30 us (54%)
  Pallas kernels  16.3 us (30%)
  waiting for transfers between devices  8.18 us (15%)
    ppermute x2, starting transfers between devices, per_device(): arrived.append(on_chip(lax.ppermute(moved, 'depth', pairs)))  11.5 us
    ppermute x4, starting transfers between devices, per_device(): back[k] = on_chip(lax.ppermute(value, ('depth', 'tile'), pairs))  8.65 us
    pallas_call x2, Pallas kernels, per_device(): pl.pallas_call(functools.partial(second_kernel, ks, pair), out_shape=[cod...  7.84 us
    ppermute x3, waiting for transfers between devices, per_device(): brought.append(on_chip(lax.ppermute(packed[k], 'tile', turned(k))))  6.11 us
    ppermute x3, starting transfers between devices, per_device(): brought.append(on_chip(lax.ppermute(packed[k], 'tile', turned(k))))  5.04 us
    pallas_call x2, Pallas kernels, per_device(): pl.pallas_call(functools.partial(unpack_kernel, tiles, pair, ks, g == 0),...  3.6 us
    ppermute x1, starting transfers between devices, per_device(): lax.ppermute(object_slices, 'depth', [((d + 1) % depths, d) for d in rang...  3.36 us
    pallas_call x1, Pallas kernels, per_device(): pl.pallas_call(functools.partial(pack_kernel, tiles, pair), out_shape=[co...  2.05 us
  transfers between devices with their start and end apart: 11, of which 4 were waited for; matrix products, arithmetic and copies ran while one was open for 0% of the time, Pallas kernels for 27%

profile of v3, /device:TPU:0, one launch (start us, length us, event | category | flops | bytes accessed | tf_op | source)
XLA Modules:
  0.0 54.7 jit_solution(7886609797033495926)
XLA Ops:
  0.0 3.4 %collective-permute-start.1 = (bf16[2,2,384,384]{3,2,1,0:T(8,128)(2,1)}, bf16[2,2,384,384]{3,2,1,0:T(8,128)(2,1)S(1)}, u32[]{:S(2)}, u32[]{:S(2)}) collective-permute-start(bf16[2,2,384,384]{3,2,1,0:T(8,128)(2,1)} %slab_ref.1), channel_id=1, source_target_pairs={{4,0},{8,4},{12,8},{16,12},{20,16},{24,20},{28,24},{0,28},{5,1},{9... | collective-permute-start | bytes 3538952 | tf_op jit(solution)/shard_map/ppermute | solution.py:425
  3.4 1.4 %collective-permute-start = (bf16[2,2,384,384]{3,2,1,0:T(8,128)(2,1)}, bf16[2,2,384,384]{3,2,1,0:T(8,128)(2,1)S(1)}, u32[]{:S(2)}, u32[]{:S(2)}) collective-permute-start(bf16[2,2,384,384]{3,2,1,0:T(8,128)(2,1)} %slab_ref.1), channel_id=1, source_target_pairs={{0,4},{8,12},{16,20},{24,28},{1,5},{9,13},{17,21},{25,29},{2,6},{1... | collective-permute-start | bytes 3538952 | tf_op jit(solution)/shard_map/ppermute | solution.py:426
  4.7 2.1 %pack.1 = (s16[2,272,128]{2,1,0:T(8,128)(2,1)S(1)}, s16[2,272,128]{2,1,0:T(8,128)(2,1)S(1)}, s16[2,272,128]{2,1,0:T(8,128)(2,1)S(1)}, s16[2,272,128]{2,1,0:T(8,128)(2,1)S(1)}) custom-call(s32[1,3,8,11]{3,2,1,0:T(8,128)} %bitcast.5, s32[1,11]{1,0:T(1,128)} %bitcast.8, f32[8,2,128,128]{3,2,1,0:T(8,128)} %bitcast.4), custom_call_target="tpu_custom_call" | custom-call | tf_op jit(solution)/shard_map/pack/pallas_call | solution.py:427
  6.8 3.0 %collective-permute-start.6 = (s16[2,272,128]{2,1,0:T(8,128)(2,1)S(1)}, s16[2,272,128]{2,1,0:T(8,128)(2,1)S(1)}, u32[]{:S(2)}, u32[]{:S(2)}) collective-permute-start(s16[2,272,128]{2,1,0:T(8,128)(2,1)S(1)} %get-tuple-element.25), channel_id=1, source_target_pairs={{0,2},{1,3},{2,0},{3,1},{4,6},{5,7},{6,4},{7,5},{8,10},{9,11},{10,... | collective-permute-start | bytes 417800 | tf_op jit(solution)/shard_map/ppermute | solution.py:455
  9.8 1.0 %collective-permute-start.7 = (s16[2,272,128]{2,1,0:T(8,128)(2,1)S(1)}, s16[2,272,128]{2,1,0:T(8,128)(2,1)S(1)}, u32[]{:S(2)}, u32[]{:S(2)}) collective-permute-start(s16[2,272,128]{2,1,0:T(8,128)(2,1)S(1)} %get-tuple-element.26), channel_id=1, source_target_pairs={{0,3},{1,0},{2,1},{3,2},{4,7},{5,4},{6,5},{7,6},{8,11},{9,8},{10,9... | collective-permute-start | bytes 417800 | tf_op jit(solution)/shard_map/ppermute | solution.py:455
  10.8 1.0 %collective-permute-start.2 = (s16[2,272,128]{2,1,0:T(8,128)(2,1)S(1)}, s16[2,272,128]{2,1,0:T(8,128)(2,1)S(1)}, u32[]{:S(2)}, u32[]{:S(2)}) collective-permute-start(s16[2,272,128]{2,1,0:T(8,128)(2,1)S(1)} %get-tuple-element.22), channel_id=1, source_target_pairs={{0,1},{1,2},{2,3},{3,0},{4,5},{5,6},{6,7},{7,4},{8,9},{9,10},{10,1... | collective-permute-start | bytes 417800 | tf_op jit(solution)/shard_map/ppermute | solution.py:455
  11.8 1.5 %prep.1 = (bf16[2,2,384,384]{3,2,1,0:T(8,128)(2,1)S(1)}, bf16[768,256]{1,0:T(8,128)(2,1)S(1)}, bf16[256,768]{1,0:T(8,128)(2,1)S(1)}, f32[2,128,128]{2,1,0:T(8,128)S(1)}) custom-call(bf16[2,2,384,384]{3,2,1,0:T(8,128)(2,1)} %slab_ref.1, bf16[768,256]{1,0:T(8,128)(2,1)} %constant.4.clone.right_ref, bf16[256,768]{1,0:T(8,128)(2,1)} %constant.5.clone.left_ref, ...), custom_call_target="tpu_custom_call" | custom-call | tf_op jit(solution)/shard_map/prep/pallas_call | solution.py:437
  13.4 6.1 %collective-permute-done.6.refs_0_ = s16[2,272,128]{2,1,0:T(8,128)(2,1)S(1)} collective-permute-done((s16[2,272,128]{2,1,0:T(8,128)(2,1)S(1)}, s16[2,272,128]{2,1,0:T(8,128)(2,1)S(1)}, u32[]{:S(2)}, u32[]{:S(2)}) %collective-permute-start.6) | collective-permute-done | bytes 139296 | tf_op jit(solution)/shard_map/ppermute | solution.py:455
  19.5 0.0 collective-permute-done.7.refs_1_
  19.5 0.0 collective-permute-done.1.next_ref
  19.5 0.6 %shard_map.75 = s16[4,272,128]{2,1,0:T(8,128)(2,1)S(1)} custom-call(bf16[2,2,384,384]{3,2,1,0:T(8,128)(2,1)S(1)} %get-tuple-element.17.own_ref, bf16[2,2,384,384]{3,2,1,0:T(8,128)(2,1)S(1)} %collective-permute-done.1.next_ref, bf16[768,256]{1,0:T(8,128)(2,1)S(1)} %get-tuple-element.19.right_ref, bf16[256,768]{1,0:T(8,128)(2,1)S(1)} %get-tuple-element.20.left_ref, ...), custom_call_target="tpu_custom_call" | custom-call | flops 1610612736 | tf_op jit(solution)/shard_map/pallas_call | solution.py:469
  20.1 6.6 %collective-permute-start.8 = (s16[4,272,128]{2,1,0:T(8,128)(2,1)S(1)}, s16[4,272,128]{2,1,0:T(8,128)(2,1)S(1)}, u32[]{:S(2)}, u32[]{:S(2)}) collective-permute-start(s16[4,272,128]{2,1,0:T(8,128)(2,1)S(1)} %shard_map.75), channel_id=1, source_target_pairs={{0,8},{4,12},{8,16},{12,20},{16,24},{1,9},{5,13},{9,17},{13,21},{1... | collective-permute-start | bytes 835592 | tf_op jit(solution)/shard_map/ppermute | solution.py:479
  26.7 0.0 collective-permute-done.2.refs_1_
  26.7 0.6 %shard_map.73 = s16[4,272,128]{2,1,0:T(8,128)(2,1)S(1)} custom-call(bf16[2,2,384,384]{3,2,1,0:T(8,128)(2,1)S(1)} %get-tuple-element.17.own_ref, bf16[2,2,384,384]{3,2,1,0:T(8,128)(2,1)S(1)} %collective-permute-done.1.next_ref, bf16[768,256]{1,0:T(8,128)(2,1)S(1)} %get-tuple-element.19.right_ref, bf16[256,768]{1,0:T(8,128)(2,1)S(1)} %get-tuple-element.20.left_ref, ...), custom_call_target="tpu_custom_call" | custom-call | flops 1610612736 | tf_op jit(solution)/shard_map/pallas_call | solution.py:469
  27.3 5.0 %collective-permute-start.3 = (s16[4,272,128]{2,1,0:T(8,128)(2,1)S(1)}, s16[4,272,128]{2,1,0:T(8,128)(2,1)S(1)}, u32[]{:S(2)}, u32[]{:S(2)}) collective-permute-start(s16[4,272,128]{2,1,0:T(8,128)(2,1)S(1)} %shard_map.73), channel_id=1, source_target_pairs={{0,8},{4,12},{8,16},{12,20},{16,24},{1,9},{5,13},{9,17},{13,21},{1... | collective-permute-start | bytes 835592 | tf_op jit(solution)/shard_map/ppermute | solution.py:479
  32.3 0.0 collective-permute-done.last_ref
  32.3 0.7 %collective-permute-done.8.arrived_ref = s16[4,272,128]{2,1,0:T(8,128)(2,1)S(1)} collective-permute-done((s16[4,272,128]{2,1,0:T(8,128)(2,1)S(1)}, s16[4,272,128]{2,1,0:T(8,128)(2,1)S(1)}, u32[]{:S(2)}, u32[]{:S(2)}) %collective-permute-start.8) | collective-permute-done | bytes 278560 | tf_op jit(solution)/shard_map/ppermute | solution.py:479
  33.0 3.7 %shard_map.76 = (s16[2,272,128]{2,1,0:T(8,128)(2,1)S(1)}, s16[2,272,128]{2,1,0:T(8,128)(2,1)S(1)}) custom-call(bf16[2,2,384,384]{3,2,1,0:T(8,128)(2,1)S(1)} %collective-permute-done.last_ref, bf16[2,2,384,384]{3,2,1,0:T(8,128)(2,1)S(1)} %get-tuple-element.17.own_ref, bf16[2,2,384,384]{3,2,1,0:T(8,128)(2,1)S(1)} %collective-permute-done.1.next_ref, ...), custom_call_target="tpu_custom_call" | custom-call | flops 1610612736 | tf_op jit(solution)/shard_map/pallas_call | solution.py:482
  36.8 0.1 collective-permute-start.9
  36.8 1.5 %collective-permute-start.10 = (s16[2,272,128]{2,1,0:T(8,128)(2,1)S(1)}, s16[2,272,128]{2,1,0:T(8,128)(2,1)S(1)}, u32[]{:S(2)}, u32[]{:S(2)}) collective-permute-start(s16[2,272,128]{2,1,0:T(8,128)(2,1)S(1)} %get-tuple-element.28), channel_id=1, source_target_pairs={{0,5},{1,6},{2,7},{3,4},{4,9},{5,10},{6,11},{7,8},{8,13},{9,14},{1... | collective-permute-start | bytes 417800 | tf_op jit(solution)/shard_map/ppermute | solution.py:493
  38.3 0.0 collective-permute-done.3.arrived_ref
  38.3 4.1 %shard_map.74 = (s16[2,272,128]{2,1,0:T(8,128)(2,1)S(1)}, s16[2,272,128]{2,1,0:T(8,128)(2,1)S(1)}) custom-call(bf16[2,2,384,384]{3,2,1,0:T(8,128)(2,1)S(1)} %collective-permute-done.last_ref, bf16[2,2,384,384]{3,2,1,0:T(8,128)(2,1)S(1)} %get-tuple-element.17.own_ref, bf16[2,2,384,384]{3,2,1,0:T(8,128)(2,1)S(1)} %collective-permute-done.1.next_ref, ...), custom_call_target="tpu_custom_call" | custom-call | flops 1610612736 | tf_op jit(solution)/shard_map/pallas_call | solution.py:482
  42.4 3.0 %collective-permute-start.4 = (s16[2,272,128]{2,1,0:T(8,128)(2,1)S(1)}, s16[2,272,128]{2,1,0:T(8,128)(2,1)S(1)}, u32[]{:S(2)}, u32[]{:S(2)}) collective-permute-start(s16[2,272,128]{2,1,0:T(8,128)(2,1)S(1)} %get-tuple-element.23), channel_id=1, source_target_pairs={{0,4},{1,5},{2,6},{3,7},{4,8},{5,9},{6,10},{7,11},{8,12},{9,13},{1... | collective-permute-start | bytes 417800 | tf_op jit(solution)/shard_map/ppermute | solution.py:493
  45.4 4.1 %collective-permute-start.5 = (s16[2,272,128]{2,1,0:T(8,128)(2,1)S(1)}, s16[2,272,128]{2,1,0:T(8,128)(2,1)S(1)}, u32[]{:S(2)}, u32[]{:S(2)}) collective-permute-start(s16[2,272,128]{2,1,0:T(8,128)(2,1)S(1)} %get-tuple-element.24), channel_id=1, source_target_pairs={{0,7},{1,4},{2,5},{3,6},{4,11},{5,8},{6,9},{7,10},{8,15},{9,12},{1... | collective-permute-start | bytes 417800 | tf_op jit(solution)/shard_map/ppermute | solution.py:493
  49.5 0.0 collective-permute-done.9.refs_0_
  49.5 0.5 collective-permute-done.10.refs_1_
  50.0 1.9 %shard_map.77.refs_2_ = f32[8,2,128,128]{3,2,1,0:T(8,128)} custom-call(s32[1,3,8,11]{3,2,1,0:T(8,128)} %bitcast.6, s32[1,11]{1,0:T(1,128)} %bitcast.9, s16[2,272,128]{2,1,0:T(8,128)(2,1)S(1)} %collective-permute-done.9.refs_0_, s16[2,272,128]{2,1,0:T(8,128)(2,1)S(1)} %collective-permute-done.10.refs_1_), custom_call_target="tpu_custom_call" | custom-call | tf_op jit(solution)/shard_map/pallas_call | solution.py:497
  51.9 0.0 collective-permute-done.4.refs_0_
  51.9 0.9 %collective-permute-done.5.refs_1_ = s16[2,272,128]{2,1,0:T(8,128)(2,1)S(1)} collective-permute-done((s16[2,272,128]{2,1,0:T(8,128)(2,1)S(1)}, s16[2,272,128]{2,1,0:T(8,128)(2,1)S(1)}, u32[]{:S(2)}, u32[]{:S(2)}) %collective-permute-start.5) | collective-permute-done | bytes 139296 | tf_op jit(solution)/shard_map/ppermute | solution.py:493
  52.8 1.7 %shard_map.78 = f32[8,2,128,128]{3,2,1,0:T(8,128)} custom-call(s32[1,3,8,11]{3,2,1,0:T(8,128)} %bitcast.7, s32[1,11]{1,0:T(1,128)} %bitcast.10, s16[2,272,128]{2,1,0:T(8,128)(2,1)S(1)} %collective-permute-done.4.refs_0_, s16[2,272,128]{2,1,0:T(8,128)(2,1)S(1)} %collective-permute-done.5.refs_1_, ...), custom_call_target="tpu_custom_call", output_to_operand_aliasing={{}: (4, {})} | custom-call | tf_op jit(solution)/shard_map/pallas_call | solution.py:497
Async XLA Ops:
  0.0 19.5 %collective-permute-start.1 = (bf16[2,2,384,384]{3,2,1,0:T(8,128)(2,1)}, bf16[2,2,384,384]{3,2,1,0:T(8,128)(2,1)S(1)}, u32[]{:S(2)}, u32[]{:S(2)}) collective-permute-start(bf16[2,2,384,384]{3,2,1,0:T(8,128)(2,1)} %slab_ref.1), channel_id=1, source_target_pairs={{4,0},{8,4},{12,8},{16,12},{20,16},{24,20},{28,24},{0,28},{5,1},{9... | collective-permute-start | bytes 3538952 | tf_op jit(solution)/shard_map/ppermute | solution.py:425
  3.4 29.0 %collective-permute-start = (bf16[2,2,384,384]{3,2,1,0:T(8,128)(2,1)}, bf16[2,2,384,384]{3,2,1,0:T(8,128)(2,1)S(1)}, u32[]{:S(2)}, u32[]{:S(2)}) collective-permute-start(bf16[2,2,384,384]{3,2,1,0:T(8,128)(2,1)} %slab_ref.1), channel_id=1, source_target_pairs={{0,4},{8,12},{16,20},{24,28},{1,5},{9,13},{17,21},{25,29},{2,6},{1... | collective-permute-start | bytes 3538952 | tf_op jit(solution)/shard_map/ppermute | solution.py:426
  6.8 12.7 %collective-permute-start.6 = (s16[2,272,128]{2,1,0:T(8,128)(2,1)S(1)}, s16[2,272,128]{2,1,0:T(8,128)(2,1)S(1)}, u32[]{:S(2)}, u32[]{:S(2)}) collective-permute-start(s16[2,272,128]{2,1,0:T(8,128)(2,1)S(1)} %get-tuple-element.25), channel_id=1, source_target_pairs={{0,2},{1,3},{2,0},{3,1},{4,6},{5,7},{6,4},{7,5},{8,10},{9,11},{10,... | collective-permute-start | bytes 417800 | tf_op jit(solution)/shard_map/ppermute | solution.py:455
  9.8 9.7 %collective-permute-start.7 = (s16[2,272,128]{2,1,0:T(8,128)(2,1)S(1)}, s16[2,272,128]{2,1,0:T(8,128)(2,1)S(1)}, u32[]{:S(2)}, u32[]{:S(2)}) collective-permute-start(s16[2,272,128]{2,1,0:T(8,128)(2,1)S(1)} %get-tuple-element.26), channel_id=1, source_target_pairs={{0,3},{1,0},{2,1},{3,2},{4,7},{5,4},{6,5},{7,6},{8,11},{9,8},{10,9... | collective-permute-start | bytes 417800 | tf_op jit(solution)/shard_map/ppermute | solution.py:455
  10.8 15.9 %collective-permute-start.2 = (s16[2,272,128]{2,1,0:T(8,128)(2,1)S(1)}, s16[2,272,128]{2,1,0:T(8,128)(2,1)S(1)}, u32[]{:S(2)}, u32[]{:S(2)}) collective-permute-start(s16[2,272,128]{2,1,0:T(8,128)(2,1)S(1)} %get-tuple-element.22), channel_id=1, source_target_pairs={{0,1},{1,2},{2,3},{3,0},{4,5},{5,6},{6,7},{7,4},{8,9},{9,10},{10,1... | collective-permute-start | bytes 417800 | tf_op jit(solution)/shard_map/ppermute | solution.py:455
  20.1 12.9 %collective-permute-start.8 = (s16[4,272,128]{2,1,0:T(8,128)(2,1)S(1)}, s16[4,272,128]{2,1,0:T(8,128)(2,1)S(1)}, u32[]{:S(2)}, u32[]{:S(2)}) collective-permute-start(s16[4,272,128]{2,1,0:T(8,128)(2,1)S(1)} %shard_map.75), channel_id=1, source_target_pairs={{0,8},{4,12},{8,16},{12,20},{16,24},{1,9},{5,13},{9,17},{13,21},{1... | collective-permute-start | bytes 835592 | tf_op jit(solution)/shard_map/ppermute | solution.py:479
  27.3 11.0 %collective-permute-start.3 = (s16[4,272,128]{2,1,0:T(8,128)(2,1)S(1)}, s16[4,272,128]{2,1,0:T(8,128)(2,1)S(1)}, u32[]{:S(2)}, u32[]{:S(2)}) collective-permute-start(s16[4,272,128]{2,1,0:T(8,128)(2,1)S(1)} %shard_map.73), channel_id=1, source_target_pairs={{0,8},{4,12},{8,16},{12,20},{16,24},{1,9},{5,13},{9,17},{13,21},{1... | collective-permute-start | bytes 835592 | tf_op jit(solution)/shard_map/ppermute | solution.py:479
  36.8 12.8 %collective-permute-start.9 = (s16[2,272,128]{2,1,0:T(8,128)(2,1)S(1)}, s16[2,272,128]{2,1,0:T(8,128)(2,1)S(1)}, u32[]{:S(2)}, u32[]{:S(2)}) collective-permute-start(s16[2,272,128]{2,1,0:T(8,128)(2,1)S(1)} %get-tuple-element.27), channel_id=1, source_target_pairs={{0,6},{1,7},{2,4},{3,5},{4,10},{5,11},{6,8},{7,9},{8,14},{9,15},{1... | collective-permute-start | bytes 417800 | tf_op jit(solution)/shard_map/ppermute | solution.py:493
  36.8 13.2 %collective-permute-start.10 = (s16[2,272,128]{2,1,0:T(8,128)(2,1)S(1)}, s16[2,272,128]{2,1,0:T(8,128)(2,1)S(1)}, u32[]{:S(2)}, u32[]{:S(2)}) collective-permute-start(s16[2,272,128]{2,1,0:T(8,128)(2,1)S(1)} %get-tuple-element.28), channel_id=1, source_target_pairs={{0,5},{1,6},{2,7},{3,4},{4,9},{5,10},{6,11},{7,8},{8,13},{9,14},{1... | collective-permute-start | bytes 417800 | tf_op jit(solution)/shard_map/ppermute | solution.py:493
  42.4 9.5 %collective-permute-start.4 = (s16[2,272,128]{2,1,0:T(8,128)(2,1)S(1)}, s16[2,272,128]{2,1,0:T(8,128)(2,1)S(1)}, u32[]{:S(2)}, u32[]{:S(2)}) collective-permute-start(s16[2,272,128]{2,1,0:T(8,128)(2,1)S(1)} %get-tuple-element.23), channel_id=1, source_target_pairs={{0,4},{1,5},{2,6},{3,7},{4,8},{5,9},{6,10},{7,11},{8,12},{9,13},{1... | collective-permute-start | bytes 417800 | tf_op jit(solution)/shard_map/ppermute | solution.py:493
  45.4 7.4 %collective-permute-start.5 = (s16[2,272,128]{2,1,0:T(8,128)(2,1)S(1)}, s16[2,272,128]{2,1,0:T(8,128)(2,1)S(1)}, u32[]{:S(2)}, u32[]{:S(2)}) collective-permute-start(s16[2,272,128]{2,1,0:T(8,128)(2,1)S(1)} %get-tuple-element.24), channel_id=1, source_target_pairs={{0,7},{1,4},{2,5},{3,6},{4,11},{5,8},{6,9},{7,10},{8,15},{9,12},{1... | collective-permute-start | bytes 417800 | tf_op jit(solution)/shard_map/ppermute | solution.py:493

commit v4 on v3

--- a/solution.py
+++ b/solution.py
@@ -22,7 +22,6 @@
 HBM = pl.BlockSpec(memory_space=pltpu.MemorySpace.HBM)
 VMEM = pl.BlockSpec(memory_space=pltpu.VMEM)
 PARAMS = pltpu.CompilerParams(vmem_limit_bytes=24 * 2**20)
-SMEM = pl.BlockSpec(memory_space=pltpu.SMEM)
 
 
 def halves(table):
@@ -108,18 +107,25 @@
         copy.wait()
 
 
-def pack_kernel(tiles, pair, list_ref, count_ref, fronts_ref, *refs):
+def pack_kernel(tiles, pair, lists_ref, counts_ref, fronts_ref, *refs):
     out_refs = refs[:tiles]
-    front_ref, in_sems = refs[tiles:]
+    front_ref, in_sems, list_ref, count_ref, list_sems = refs[tiles:]
     slots, _, width, _ = fronts_ref.shape
     own = lax.axis_index("tile")
-    starting = batches()[0]
 
     def fetch(p):
         return pltpu.make_async_copy(fronts_ref.at[p], front_ref.at[p], in_sems.at[p])
 
+    lists = [
+        pltpu.make_async_copy(lists_ref, list_ref, list_sems.at[0]),
+        pltpu.make_async_copy(counts_ref, count_ref, list_sems.at[1]),
+    ]
+    for copy in lists:
+        copy.start()
     for p in range(slots):
-        pl.when(p < count_ref[0, starting])(lambda p=p: fetch(p).start())
+        fetch(p).start()
+    for copy in lists:
+        copy.wait()
     chosen = {}
     for k in range(tiles):
         tile = lax.rem(own + k, tiles)
@@ -129,7 +135,7 @@
                     lambda p: list_ref[0, 0, p, batch], count_ref[0, batch], slots, tile, i
                 )
     for p in range(slots):
-        pl.when(p < count_ref[0, starting])(lambda p=p: fetch(p).wait())
+        fetch(p).wait()
     lane = lax.broadcasted_iota(jnp.int32, (1, width), 1)
     for k in list(range(1, tiles)) + [0]:
         for i in range(pair):
@@ -157,8 +163,16 @@
                 store(2 * width, extra_rows((none, none), places))
 
 
-def unpack_kernel(tiles, pair, ks, first, list_ref, count_ref, *refs):
-    in_refs, (out_ref, exit_ref, out_sems) = refs[: len(ks)], refs[-3:]
+def unpack_kernel(tiles, pair, ks, first, lists_ref, counts_ref, *refs):
+    in_refs, (out_ref, exit_ref, out_sems, list_ref, count_ref, list_sems) = refs[: len(ks)], refs[-6:]
+    lists = [
+        pltpu.make_async_copy(lists_ref, list_ref, list_sems.at[0]),
+        pltpu.make_async_copy(counts_ref, count_ref, list_sems.at[1]),
+    ]
+    for copy in lists:
+        copy.start()
+    for copy in lists:
+        copy.wait()
     slots, _, width, _ = out_ref.shape
     own = lax.axis_index("tile")
     batch = lax.axis_size("depth") + STEPS - 2 - lax.axis_index("depth")
@@ -427,9 +441,14 @@
     packed = pl.pallas_call(
         functools.partial(pack_kernel, tiles, pair),
         out_shape=[coded] * tiles,
-        in_specs=[SMEM, SMEM, HBM],
+        in_specs=[HBM, HBM, HBM],
         out_specs=[VMEM] * tiles,
-        scratch_shapes=[pltpu.VMEM(fronts.shape[2:], jnp.float32), pltpu.SemaphoreType.DMA((slots,))],
+        scratch_shapes=[
+            pltpu.VMEM(fronts.shape[2:], jnp.float32),
+            pltpu.SemaphoreType.DMA((slots,)),
+            *[pltpu.SMEM(value.shape, jnp.int32) for value in lists],
+            pltpu.SemaphoreType.DMA((2,)),
+        ],
         compiler_params=PARAMS,
         name="pack",
     )(*lists, off_chip(fronts[0, 0]))
@@ -497,10 +516,15 @@
         exits = pl.pallas_call(
             functools.partial(unpack_kernel, tiles, pair, ks, g == 0),
             out_shape=jax.ShapeDtypeStruct(fronts.shape[2:], jnp.float32),
-            in_specs=[SMEM, SMEM] + [VMEM] * per_group + [HBM] * len(before),
+            in_specs=[HBM, HBM] + [VMEM] * per_group + [HBM] * len(before),
             out_specs=HBM,
             input_output_aliases={2 + per_group: 0} if before else {},
-            scratch_shapes=[pltpu.VMEM(fronts.shape[2:], jnp.float32), pltpu.SemaphoreType.DMA((slots,))],
+            scratch_shapes=[
+                pltpu.VMEM(fronts.shape[2:], jnp.float32),
+                pltpu.SemaphoreType.DMA((slots,)),
+                *[pltpu.SMEM(value.shape, jnp.int32) for value in lists],
+                pltpu.SemaphoreType.DMA((2,)),
+            ],
             compiler_params=PARAMS,
         )(*lists, *[back[k] for k in ks], *before)
     return exits[None, None]

time: 55.1 us -> 54 us (0.980)
  the two profiles are of different devices: /device:TPU:0 before, /device:TPU:20 now
where the time goes in v4:
time: 54 us; the launch traced here: 53.7 us
  waiting for transfers between devices  19.1 us (35%)
  Pallas kernels  18.7 us (35%)
  starting transfers between devices  15.6 us (29%)
    ppermute x4, waiting for transfers between devices, per_device(): back[k] = on_chip(lax.ppermute(value, ('depth', 'tile'), pairs))  8.32 us
    pallas_call x2, Pallas kernels, per_device(): pl.pallas_call(functools.partial(first_kernel, ks, pair), out_shape=moved...  7.35 us
    ppermute x3, waiting for transfers between devices, per_device(): brought.append(on_chip(lax.ppermute(packed[k], 'tile', turned(k))))  6.95 us
    ppermute x4, starting transfers between devices, per_device(): back[k] = on_chip(lax.ppermute(value, ('depth', 'tile'), pairs))  6.06 us
    pallas_call x2, Pallas kernels, per_device(): pl.pallas_call(functools.partial(second_kernel, ks, pair), out_shape=[cod...  4.54 us
    ppermute x2, starting transfers between devices, per_device(): arrived.append(on_chip(lax.ppermute(moved, 'depth', pairs)))  3.84 us
    ppermute x2, waiting for transfers between devices, per_device(): arrived.append(on_chip(lax.ppermute(moved, 'depth', pairs)))  3.79 us
    pallas_call x2, Pallas kernels, per_device(): pl.pallas_call(functools.partial(unpack_kernel, tiles, pair, ks, g == 0),...  3.63 us
  transfers between devices with their start and end apart: 11, of which 6 were waited for; matrix products, arithmetic and copies ran while one was open for 0% of the time, Pallas kernels for 32%

profile of v4, /device:TPU:20, one launch (start us, length us, event | category | flops | bytes accessed | tf_op | source)
XLA Modules:
  0.0 53.7 jit_solution(16866708363200860846)
XLA Ops:
  0.0 0.9 %collective-permute-start.1 = (bf16[2,2,384,384]{3,2,1,0:T(8,128)(2,1)}, bf16[2,2,384,384]{3,2,1,0:T(8,128)(2,1)S(1)}, u32[]{:S(2)}, u32[]{:S(2)}) collective-permute-start(bf16[2,2,384,384]{3,2,1,0:T(8,128)(2,1)} %slab_ref.1), channel_id=1, source_target_pairs={{4,0},{8,4},{12,8},{16,12},{20,16},{24,20},{28,24},{0,28},{5,1},{9... | collective-permute-start | bytes 3538952 | tf_op jit(solution)/shard_map/ppermute | solution.py:439
  0.9 1.6 %collective-permute-start = (bf16[2,2,384,384]{3,2,1,0:T(8,128)(2,1)}, bf16[2,2,384,384]{3,2,1,0:T(8,128)(2,1)S(1)}, u32[]{:S(2)}, u32[]{:S(2)}) collective-permute-start(bf16[2,2,384,384]{3,2,1,0:T(8,128)(2,1)} %slab_ref.1), channel_id=1, source_target_pairs={{0,4},{8,12},{16,20},{24,28},{1,5},{9,13},{17,21},{25,29},{2,6},{1... | collective-permute-start | bytes 3538952 | tf_op jit(solution)/shard_map/ppermute | solution.py:440
  2.5 1.7 %pack.1 = (s16[2,272,128]{2,1,0:T(8,128)(2,1)S(1)}, s16[2,272,128]{2,1,0:T(8,128)(2,1)S(1)}, s16[2,272,128]{2,1,0:T(8,128)(2,1)S(1)}, s16[2,272,128]{2,1,0:T(8,128)(2,1)S(1)}) custom-call(s32[1,3,8,11]{3,2,1,0:T(8,128)} %bitcast.5, s32[1,11]{1,0:T(1,128)} %bitcast.8, f32[8,2,128,128]{3,2,1,0:T(8,128)} %bitcast.4), custom_call_target="tpu_custom_call" | custom-call | tf_op jit(solution)/shard_map/pack/pallas_call | solution.py:441
  4.1 0.4 collective-permute-start.6
  4.5 2.9 %collective-permute-start.7 = (s16[2,272,128]{2,1,0:T(8,128)(2,1)S(1)}, s16[2,272,128]{2,1,0:T(8,128)(2,1)S(1)}, u32[]{:S(2)}, u32[]{:S(2)}) collective-permute-start(s16[2,272,128]{2,1,0:T(8,128)(2,1)S(1)} %get-tuple-element.26), channel_id=1, source_target_pairs={{0,3},{1,0},{2,1},{3,2},{4,7},{5,4},{6,5},{7,6},{8,11},{9,8},{10,9... | collective-permute-start | bytes 417800 | tf_op jit(solution)/shard_map/ppermute | solution.py:474
  7.4 0.0 collective-permute-start.2
  7.4 1.5 %prep.1 = (bf16[2,2,384,384]{3,2,1,0:T(8,128)(2,1)S(1)}, bf16[768,256]{1,0:T(8,128)(2,1)S(1)}, bf16[256,768]{1,0:T(8,128)(2,1)S(1)}, f32[2,128,128]{2,1,0:T(8,128)S(1)}) custom-call(bf16[2,2,384,384]{3,2,1,0:T(8,128)(2,1)} %slab_ref.1, bf16[768,256]{1,0:T(8,128)(2,1)} %constant.4.clone.right_ref, bf16[256,768]{1,0:T(8,128)(2,1)} %constant.5.clone.left_ref, ...), custom_call_target="tpu_custom_call" | custom-call | tf_op jit(solution)/shard_map/prep/pallas_call | solution.py:456
  8.9 3.4 %collective-permute-done.6.refs_0_ = s16[2,272,128]{2,1,0:T(8,128)(2,1)S(1)} collective-permute-done((s16[2,272,128]{2,1,0:T(8,128)(2,1)S(1)}, s16[2,272,128]{2,1,0:T(8,128)(2,1)S(1)}, u32[]{:S(2)}, u32[]{:S(2)}) %collective-permute-start.6) | collective-permute-done | bytes 139296 | tf_op jit(solution)/shard_map/ppermute | solution.py:474
  12.3 3.6 %collective-permute-done.7.refs_1_ = s16[2,272,128]{2,1,0:T(8,128)(2,1)S(1)} collective-permute-done((s16[2,272,128]{2,1,0:T(8,128)(2,1)S(1)}, s16[2,272,128]{2,1,0:T(8,128)(2,1)S(1)}, u32[]{:S(2)}, u32[]{:S(2)}) %collective-permute-start.7) | collective-permute-done | bytes 139296 | tf_op jit(solution)/shard_map/ppermute | solution.py:474
  15.9 0.0 collective-permute-done.1.next_ref
  15.9 3.7 %shard_map.75 = s16[4,272,128]{2,1,0:T(8,128)(2,1)S(1)} custom-call(bf16[2,2,384,384]{3,2,1,0:T(8,128)(2,1)S(1)} %get-tuple-element.17.own_ref, bf16[2,2,384,384]{3,2,1,0:T(8,128)(2,1)S(1)} %collective-permute-done.1.next_ref, bf16[768,256]{1,0:T(8,128)(2,1)S(1)} %get-tuple-element.19.right_ref, bf16[256,768]{1,0:T(8,128)(2,1)S(1)} %get-tuple-element.20.left_ref, ...), custom_call_target="tpu_custom_call" | custom-call | flops 1610612736 | tf_op jit(solution)/shard_map/pallas_call | solution.py:488
  19.6 1.9 %collective-permute-start.8 = (s16[4,272,128]{2,1,0:T(8,128)(2,1)S(1)}, s16[4,272,128]{2,1,0:T(8,128)(2,1)S(1)}, u32[]{:S(2)}, u32[]{:S(2)}) collective-permute-start(s16[4,272,128]{2,1,0:T(8,128)(2,1)S(1)} %shard_map.75), channel_id=1, source_target_pairs={{0,8},{4,12},{8,16},{12,20},{16,24},{1,9},{5,13},{9,17},{13,21},{1... | collective-permute-start | bytes 835592 | tf_op jit(solution)/shard_map/ppermute | solution.py:498
  21.5 0.0 collective-permute-done.2.refs_1_
  21.5 3.7 %shard_map.73 = s16[4,272,128]{2,1,0:T(8,128)(2,1)S(1)} custom-call(bf16[2,2,384,384]{3,2,1,0:T(8,128)(2,1)S(1)} %get-tuple-element.17.own_ref, bf16[2,2,384,384]{3,2,1,0:T(8,128)(2,1)S(1)} %collective-permute-done.1.next_ref, bf16[768,256]{1,0:T(8,128)(2,1)S(1)} %get-tuple-element.19.right_ref, bf16[256,768]{1,0:T(8,128)(2,1)S(1)} %get-tuple-element.20.left_ref, ...), custom_call_target="tpu_custom_call" | custom-call | flops 1610612736 | tf_op jit(solution)/shard_map/pallas_call | solution.py:488
  25.2 1.9 %collective-permute-start.3 = (s16[4,272,128]{2,1,0:T(8,128)(2,1)S(1)}, s16[4,272,128]{2,1,0:T(8,128)(2,1)S(1)}, u32[]{:S(2)}, u32[]{:S(2)}) collective-permute-start(s16[4,272,128]{2,1,0:T(8,128)(2,1)S(1)} %shard_map.73), channel_id=1, source_target_pairs={{0,8},{4,12},{8,16},{12,20},{16,24},{1,9},{5,13},{9,17},{13,21},{1... | collective-permute-start | bytes 835592 | tf_op jit(solution)/shard_map/ppermute | solution.py:498
  27.1 0.0 collective-permute-done.last_ref
  27.1 3.7 %collective-permute-done.8.arrived_ref = s16[4,272,128]{2,1,0:T(8,128)(2,1)S(1)} collective-permute-done((s16[4,272,128]{2,1,0:T(8,128)(2,1)S(1)}, s16[4,272,128]{2,1,0:T(8,128)(2,1)S(1)}, u32[]{:S(2)}, u32[]{:S(2)}) %collective-permute-start.8) | collective-permute-done | bytes 278560 | tf_op jit(solution)/shard_map/ppermute | solution.py:498
  30.8 3.7 %shard_map.76 = (s16[2,272,128]{2,1,0:T(8,128)(2,1)S(1)}, s16[2,272,128]{2,1,0:T(8,128)(2,1)S(1)}) custom-call(bf16[2,2,384,384]{3,2,1,0:T(8,128)(2,1)S(1)} %collective-permute-done.last_ref, bf16[2,2,384,384]{3,2,1,0:T(8,128)(2,1)S(1)} %get-tuple-element.17.own_ref, bf16[2,2,384,384]{3,2,1,0:T(8,128)(2,1)S(1)} %collective-permute-done.1.next_ref, ...), custom_call_target="tpu_custom_call" | custom-call | flops 1610612736 | tf_op jit(solution)/shard_map/pallas_call | solution.py:501
  34.5 0.1 collective-permute-start.9
  34.6 0.4 collective-permute-start.10
  35.0 0.1 collective-permute-done.3.arrived_ref
  35.1 0.8 %shard_map.74 = (s16[2,272,128]{2,1,0:T(8,128)(2,1)S(1)}, s16[2,272,128]{2,1,0:T(8,128)(2,1)S(1)}) custom-call(bf16[2,2,384,384]{3,2,1,0:T(8,128)(2,1)S(1)} %collective-permute-done.last_ref, bf16[2,2,384,384]{3,2,1,0:T(8,128)(2,1)S(1)} %get-tuple-element.17.own_ref, bf16[2,2,384,384]{3,2,1,0:T(8,128)(2,1)S(1)} %collective-permute-done.1.next_ref, ...), custom_call_target="tpu_custom_call" | custom-call | flops 1610612736 | tf_op jit(solution)/shard_map/pallas_call | solution.py:501
  35.9 2.5 %collective-permute-start.4 = (s16[2,272,128]{2,1,0:T(8,128)(2,1)S(1)}, s16[2,272,128]{2,1,0:T(8,128)(2,1)S(1)}, u32[]{:S(2)}, u32[]{:S(2)}) collective-permute-start(s16[2,272,128]{2,1,0:T(8,128)(2,1)S(1)} %get-tuple-element.23), channel_id=1, source_target_pairs={{0,4},{1,5},{2,6},{3,7},{4,8},{5,9},{6,10},{7,11},{8,12},{9,13},{1... | collective-permute-start | bytes 417800 | tf_op jit(solution)/shard_map/ppermute | solution.py:512
  38.5 3.1 %collective-permute-start.5 = (s16[2,272,128]{2,1,0:T(8,128)(2,1)S(1)}, s16[2,272,128]{2,1,0:T(8,128)(2,1)S(1)}, u32[]{:S(2)}, u32[]{:S(2)}) collective-permute-start(s16[2,272,128]{2,1,0:T(8,128)(2,1)S(1)} %get-tuple-element.24), channel_id=1, source_target_pairs={{0,7},{1,4},{2,5},{3,6},{4,11},{5,8},{6,9},{7,10},{8,15},{9,12},{1... | collective-permute-start | bytes 417800 | tf_op jit(solution)/shard_map/ppermute | solution.py:512
  41.5 1.1 %collective-permute-done.9.refs_0_ = s16[2,272,128]{2,1,0:T(8,128)(2,1)S(1)} collective-permute-done((s16[2,272,128]{2,1,0:T(8,128)(2,1)S(1)}, s16[2,272,128]{2,1,0:T(8,128)(2,1)S(1)}, u32[]{:S(2)}, u32[]{:S(2)}) %collective-permute-start.9) | collective-permute-done | bytes 139296 | tf_op jit(solution)/shard_map/ppermute | solution.py:512
  42.7 7.2 %collective-permute-done.10.refs_1_ = s16[2,272,128]{2,1,0:T(8,128)(2,1)S(1)} collective-permute-done((s16[2,272,128]{2,1,0:T(8,128)(2,1)S(1)}, s16[2,272,128]{2,1,0:T(8,128)(2,1)S(1)}, u32[]{:S(2)}, u32[]{:S(2)}) %collective-permute-start.10) | collective-permute-done | bytes 139296 | tf_op jit(solution)/shard_map/ppermute | solution.py:512
  49.9 1.9 %shard_map.77.refs_2_ = f32[8,2,128,128]{3,2,1,0:T(8,128)} custom-call(s32[1,3,8,11]{3,2,1,0:T(8,128)} %bitcast.6, s32[1,11]{1,0:T(1,128)} %bitcast.9, s16[2,272,128]{2,1,0:T(8,128)(2,1)S(1)} %collective-permute-done.9.refs_0_, s16[2,272,128]{2,1,0:T(8,128)(2,1)S(1)} %collective-permute-done.10.refs_1_), custom_call_target="tpu_custom_call" | custom-call | tf_op jit(solution)/shard_map/pallas_call | solution.py:516
  51.8 0.0 collective-permute-done.4.refs_0_
  51.8 0.0 collective-permute-done.5.refs_1_
  51.8 1.7 %shard_map.78 = f32[8,2,128,128]{3,2,1,0:T(8,128)} custom-call(s32[1,3,8,11]{3,2,1,0:T(8,128)} %bitcast.7, s32[1,11]{1,0:T(1,128)} %bitcast.10, s16[2,272,128]{2,1,0:T(8,128)(2,1)S(1)} %collective-permute-done.4.refs_0_, s16[2,272,128]{2,1,0:T(8,128)(2,1)S(1)} %collective-permute-done.5.refs_1_, ...), custom_call_target="tpu_custom_call", output_to_operand_aliasing={{}: (4, {})} | custom-call | tf_op jit(solution)/shard_map/pallas_call | solution.py:516
Async XLA Ops:
  0.0 15.9 %collective-permute-start.1 = (bf16[2,2,384,384]{3,2,1,0:T(8,128)(2,1)}, bf16[2,2,384,384]{3,2,1,0:T(8,128)(2,1)S(1)}, u32[]{:S(2)}, u32[]{:S(2)}) collective-permute-start(bf16[2,2,384,384]{3,2,1,0:T(8,128)(2,1)} %slab_ref.1), channel_id=1, source_target_pairs={{4,0},{8,4},{12,8},{16,12},{20,16},{24,20},{28,24},{0,28},{5,1},{9... | collective-permute-start | bytes 3538952 | tf_op jit(solution)/shard_map/ppermute | solution.py:439
  0.9 26.2 %collective-permute-start = (bf16[2,2,384,384]{3,2,1,0:T(8,128)(2,1)}, bf16[2,2,384,384]{3,2,1,0:T(8,128)(2,1)S(1)}, u32[]{:S(2)}, u32[]{:S(2)}) collective-permute-start(bf16[2,2,384,384]{3,2,1,0:T(8,128)(2,1)} %slab_ref.1), channel_id=1, source_target_pairs={{0,4},{8,12},{16,20},{24,28},{1,5},{9,13},{17,21},{25,29},{2,6},{1... | collective-permute-start | bytes 3538952 | tf_op jit(solution)/shard_map/ppermute | solution.py:440
  4.1 8.2 %collective-permute-start.6 = (s16[2,272,128]{2,1,0:T(8,128)(2,1)S(1)}, s16[2,272,128]{2,1,0:T(8,128)(2,1)S(1)}, u32[]{:S(2)}, u32[]{:S(2)}) collective-permute-start(s16[2,272,128]{2,1,0:T(8,128)(2,1)S(1)} %get-tuple-element.25), channel_id=1, source_target_pairs={{0,2},{1,3},{2,0},{3,1},{4,6},{5,7},{6,4},{7,5},{8,10},{9,11},{10,... | collective-permute-start | bytes 417800 | tf_op jit(solution)/shard_map/ppermute | solution.py:474
  4.5 11.4 %collective-permute-start.7 = (s16[2,272,128]{2,1,0:T(8,128)(2,1)S(1)}, s16[2,272,128]{2,1,0:T(8,128)(2,1)S(1)}, u32[]{:S(2)}, u32[]{:S(2)}) collective-permute-start(s16[2,272,128]{2,1,0:T(8,128)(2,1)S(1)} %get-tuple-element.26), channel_id=1, source_target_pairs={{0,3},{1,0},{2,1},{3,2},{4,7},{5,4},{6,5},{7,6},{8,11},{9,8},{10,9... | collective-permute-start | bytes 417800 | tf_op jit(solution)/shard_map/ppermute | solution.py:474
  7.4 14.1 %collective-permute-start.2 = (s16[2,272,128]{2,1,0:T(8,128)(2,1)S(1)}, s16[2,272,128]{2,1,0:T(8,128)(2,1)S(1)}, u32[]{:S(2)}, u32[]{:S(2)}) collective-permute-start(s16[2,272,128]{2,1,0:T(8,128)(2,1)S(1)} %get-tuple-element.22), channel_id=1, source_target_pairs={{0,1},{1,2},{2,3},{3,0},{4,5},{5,6},{6,7},{7,4},{8,9},{9,10},{10,1... | collective-permute-start | bytes 417800 | tf_op jit(solution)/shard_map/ppermute | solution.py:474
  19.6 11.2 %collective-permute-start.8 = (s16[4,272,128]{2,1,0:T(8,128)(2,1)S(1)}, s16[4,272,128]{2,1,0:T(8,128)(2,1)S(1)}, u32[]{:S(2)}, u32[]{:S(2)}) collective-permute-start(s16[4,272,128]{2,1,0:T(8,128)(2,1)S(1)} %shard_map.75), channel_id=1, source_target_pairs={{0,8},{4,12},{8,16},{12,20},{16,24},{1,9},{5,13},{9,17},{13,21},{1... | collective-permute-start | bytes 835592 | tf_op jit(solution)/shard_map/ppermute | solution.py:498
  25.2 9.9 %collective-permute-start.3 = (s16[4,272,128]{2,1,0:T(8,128)(2,1)S(1)}, s16[4,272,128]{2,1,0:T(8,128)(2,1)S(1)}, u32[]{:S(2)}, u32[]{:S(2)}) collective-permute-start(s16[4,272,128]{2,1,0:T(8,128)(2,1)S(1)} %shard_map.73), channel_id=1, source_target_pairs={{0,8},{4,12},{8,16},{12,20},{16,24},{1,9},{5,13},{9,17},{13,21},{1... | collective-permute-start | bytes 835592 | tf_op jit(solution)/shard_map/ppermute | solution.py:498
  34.5 8.2 %collective-permute-start.9 = (s16[2,272,128]{2,1,0:T(8,128)(2,1)S(1)}, s16[2,272,128]{2,1,0:T(8,128)(2,1)S(1)}, u32[]{:S(2)}, u32[]{:S(2)}) collective-permute-start(s16[2,272,128]{2,1,0:T(8,128)(2,1)S(1)} %get-tuple-element.27), channel_id=1, source_target_pairs={{0,6},{1,7},{2,4},{3,5},{4,10},{5,11},{6,8},{7,9},{8,14},{9,15},{1... | collective-permute-start | bytes 417800 | tf_op jit(solution)/shard_map/ppermute | solution.py:512
  34.6 15.3 %collective-permute-start.10 = (s16[2,272,128]{2,1,0:T(8,128)(2,1)S(1)}, s16[2,272,128]{2,1,0:T(8,128)(2,1)S(1)}, u32[]{:S(2)}, u32[]{:S(2)}) collective-permute-start(s16[2,272,128]{2,1,0:T(8,128)(2,1)S(1)} %get-tuple-element.28), channel_id=1, source_target_pairs={{0,5},{1,6},{2,7},{3,4},{4,9},{5,10},{6,11},{7,8},{8,13},{9,14},{1... | collective-permute-start | bytes 417800 | tf_op jit(solution)/shard_map/ppermute | solution.py:512
  35.9 15.8 %collective-permute-start.4 = (s16[2,272,128]{2,1,0:T(8,128)(2,1)S(1)}, s16[2,272,128]{2,1,0:T(8,128)(2,1)S(1)}, u32[]{:S(2)}, u32[]{:S(2)}) collective-permute-start(s16[2,272,128]{2,1,0:T(8,128)(2,1)S(1)} %get-tuple-element.23), channel_id=1, source_target_pairs={{0,4},{1,5},{2,6},{3,7},{4,8},{5,9},{6,10},{7,11},{8,12},{9,13},{1... | collective-permute-start | bytes 417800 | tf_op jit(solution)/shard_map/ppermute | solution.py:512
  38.5 13.3 %collective-permute-start.5 = (s16[2,272,128]{2,1,0:T(8,128)(2,1)S(1)}, s16[2,272,128]{2,1,0:T(8,128)(2,1)S(1)}, u32[]{:S(2)}, u32[]{:S(2)}) collective-permute-start(s16[2,272,128]{2,1,0:T(8,128)(2,1)S(1)} %get-tuple-element.24), channel_id=1, source_target_pairs={{0,7},{1,4},{2,5},{3,6},{4,11},{5,8},{6,9},{7,10},{8,15},{9,12},{1... | collective-permute-start | bytes 417800 | tf_op jit(solution)/shard_map/ppermute | solution.py:512
